TPU v7x, 32 devices: a whole 2x2x4 slice. The times are simulated.
32 devices in a mesh: scene: 2 (over x), frame: 16 (over z, y, core).
Axes of the slice: x: 2, y: 2, z: 4, core: 2. Of those that a mesh axis runs over, the one named last changes fastest.
Arguments:
- tokens: bfloat16 [2, 2304, 1024], P('scene', 'frame'), may hold values from -6 to 6
- patch_counts: int32 [2, 16], P('scene', 'frame'), may hold values from 43 to 139, as said below
- first_gain: bfloat16 [2, 1024], replicated, may hold values from 0.25 to 1.75
- first_shift: bfloat16 [2, 1024], replicated, may hold values from -3 to 3
- joint_weight: bfloat16 [2, 1024, 3072], replicated, may hold values from -0.1875 to 0.1875
- joint_bias: bfloat16 [2, 3072], replicated, may hold values from -3 to 3
- query_gain: bfloat16 [2, 64], replicated, may hold values from 0.796875 to 1.796875
- query_shift: bfloat16 [2, 64], replicated, may hold values from -3 to 3
- key_gain: bfloat16 [2, 64], replicated, may hold values from 0.796875 to 1.796875
- mixer_weight: bfloat16 [2, 1024, 1024], replicated, may hold values from -2 to 2
- mixer_bias: bfloat16 [2, 1024], replicated, may hold values from -3 to 3
- mixer_scale: bfloat16 [2, 1024], replicated, may hold values from 0.25 to 1.75
- second_gain: bfloat16 [2, 1024], replicated, may hold values from 0.25 to 1.75
- second_shift: bfloat16 [2, 1024], replicated, may hold values from -3 to 3
- inner_weight: bfloat16 [2, 1024, 4096], replicated, may hold values from -0.1875 to 0.1875
- inner_bias: bfloat16 [2, 4096], replicated, may hold values from -3 to 3
- outer_weight: bfloat16 [2, 4096, 1024], replicated, may hold values from -0.09375 to 0.09375
- outer_bias: bfloat16 [2, 1024], replicated, may hold values from -3 to 3
- outer_scale: bfloat16 [2, 1024], replicated, may hold values from 0.25 to 1.75
- cotangent: bfloat16 [2, 2304, 1024], P('scene', 'frame'), may hold values from -6 to 6
Outputs:
- layer_out: bfloat16 [2, 2304, 1024], P('scene', 'frame')
- grad_tokens: bfloat16 [2, 2304, 1024], P('scene', 'frame')
- grad_first_gain: float32 [2, 1024], replicated
- grad_first_shift: float32 [2, 1024], replicated
- grad_joint_weight: float32 [2, 1024, 3072], P(None, ('scene', 'frame'))
- grad_joint_bias: float32 [2, 3072], replicated
- grad_query_gain: float32 [2, 64], replicated
- grad_query_shift: float32 [2, 64], replicated
- grad_key_gain: float32 [2, 64], replicated
- grad_mixer_weight: float32 [2, 1024, 1024], P(None, ('scene', 'frame'))
- grad_mixer_bias: float32 [2, 1024], replicated
- grad_mixer_scale: float32 [2, 1024], replicated
- grad_second_gain: float32 [2, 1024], replicated
- grad_second_shift: float32 [2, 1024], replicated
- grad_inner_weight: float32 [2, 1024, 4096], P(None, ('scene', 'frame'))
- grad_inner_bias: float32 [2, 4096], replicated
- grad_outer_weight: float32 [2, 4096, 1024], P(None, ('scene', 'frame'))
- grad_outer_bias: float32 [2, 1024], replicated
- grad_outer_scale: float32 [2, 1024], replicated
Inputs may be any that keep to these rules, and one draw needn't show every extreme that they name: `patch_counts`: A frame's 5 camera and register tokens and then its patches fill the first slots of its 144; in every scene some frame has the most patches and some the fewest.
All inputs are finite; a program needn't handle non-finite values.
Results may differ from a plain program's by a relative error of at most 0.014.
Values may be sent and summed in bfloat16 or wider, within the bound.
A program may use at most 384 MiB of HBM per device.

v0:
```python
from functools import partial

import jax
import jax.numpy as jnp
from jax import lax
from jax.sharding import PartitionSpec as P

SPECIAL = 5


norm_eps = 1e-06
head_eps = 1e-05
mask_depth = 1000000000.0
float_type = jnp.float32
half_type = jnp.bfloat16


def layer_norm(inputs, norm_gain, norm_shift, epsilon):
    average = jnp.mean(inputs, axis=-1, keepdims=True)
    centered = inputs - average
    variance = jnp.mean(centered * centered, axis=-1, keepdims=True)
    return centered * lax.rsqrt(variance + epsilon) * norm_gain + norm_shift


def key_norm(inputs, norm_gain):
    return layer_norm(inputs, norm_gain, 0.0, head_eps)


def gelu_exact(inputs):
    return jax.nn.gelu(inputs, approximate=False)


def matmul(left_side, right_side):
    return jnp.dot(left_side, right_side, preferred_element_type=float_type)


def matmul_back(left_side, right_side):
    return lax.dot_general(
        left_side, right_side, (((1,), (1,)), ((), ())), preferred_element_type=float_type
    )


def matmul_rows(left_side, right_side):
    return lax.dot_general(
        left_side, right_side, (((0,), (0,)), ((), ())), preferred_element_type=float_type
    )


def split_heads(flat_rows, head_count):
    return flat_rows.reshape(flat_rows.shape[0], head_count, flat_rows.shape[1] // head_count)


def raw_scores(queries, key_heads, key_bias):
    score_scale = queries.shape[-1] ** (-0.5)
    dot_scores = jnp.einsum("qhe,khe->hqk", queries, key_heads, preferred_element_type=float_type)
    return dot_scores * score_scale + key_bias[None, None, :]


def score_parts(queries, key_heads, values, key_bias, log_total, grad_out):
    probability = jnp.exp(raw_scores(queries, key_heads, key_bias) - log_total)
    grad_probs = jnp.einsum("qhe,khe->hqk", grad_out, values, preferred_element_type=float_type)
    return (probability, grad_probs)


def grads_from(queries, key_heads, probability, grad_probs, row_delta, grad_out):
    score_scale = queries.shape[-1] ** (-0.5)
    grad_scores = (probability * (grad_probs - row_delta)).astype(half_type)
    grad_queries = (
        jnp.einsum("hqk,khe->qhe", grad_scores, key_heads, preferred_element_type=float_type)
        * score_scale
    )
    grad_keys = (
        jnp.einsum("hqk,qhe->khe", grad_scores, queries, preferred_element_type=float_type)
        * score_scale
    )
    grad_values = jnp.einsum(
        "hqk,qhe->khe", probability.astype(half_type), grad_out, preferred_element_type=float_type
    )
    return (grad_queries, grad_keys, grad_values)


def block_span(total_rows, frame_rows):
    shards = total_rows // frame_rows
    group_frames = 1
    while group_frames * 2 * frame_rows <= 1024 and shards % (group_frames * 2) == 0:
        group_frames = group_frames * 2
    return group_frames * frame_rows


def as_blocks(stacked_rows, key_span):
    return stacked_rows.reshape(
        (stacked_rows.shape[0] // key_span, key_span) + stacked_rows.shape[1:]
    )


def global_forward(queries, keys_all, values_all, bias_all, key_span):
    key_parts = (
        as_blocks(keys_all, key_span),
        as_blocks(values_all, key_span),
        as_blocks(bias_all, key_span),
    )

    def norm_step(state_pair, block_part):
        running_max, running_total = state_pair
        scores = raw_scores(queries, block_part[0], block_part[2])
        new_max = jnp.maximum(running_max, jnp.max(scores, axis=-1, keepdims=True))
        running_total = running_total * jnp.exp(running_max - new_max) + jnp.sum(
            jnp.exp(scores - new_max), axis=-1, keepdims=True
        )
        return ((new_max, running_total), None)

    stat_shape = (queries.shape[1], queries.shape[0], 1)
    initial = (jnp.full(stat_shape, -jnp.inf, float_type), jnp.zeros(stat_shape, float_type))
    (running_max, running_total), _ = lax.scan(norm_step, initial, key_parts)
    log_total = running_max + jnp.log(running_total)

    def value_step(accumulated, block_part):
        probability = jnp.exp(raw_scores(queries, block_part[0], block_part[2]) - log_total).astype(
            half_type
        )
        return (
            accumulated
            + jnp.einsum(
                "hqk,khe->qhe", probability, block_part[1], preferred_element_type=float_type
            ),
            None,
        )

    attended, _ = lax.scan(value_step, jnp.zeros(queries.shape, float_type), key_parts)
    return (attended, log_total)


def scene_row_delta(queries, key_parts, log_total, grad_out):

    def delta_step(accumulated, block_part):
        probability, grad_probs = score_parts(
            queries, block_part[0], block_part[1], block_part[2], log_total, grad_out
        )
        return (accumulated + jnp.sum(probability * grad_probs, axis=-1, keepdims=True), None)

    row_delta, _ = lax.scan(delta_step, jnp.zeros(log_total.shape, float_type), key_parts)
    return row_delta


def global_backward(queries, keys_all, values_all, bias_all, log_total, grad_out, key_span):
    key_parts = (
        as_blocks(keys_all, key_span),
        as_blocks(values_all, key_span),
        as_blocks(bias_all, key_span),
    )
    row_delta = scene_row_delta(queries, key_parts, log_total, grad_out)

    def grad_step(accumulated, block_part):
        probability, grad_probs = score_parts(
            queries, block_part[0], block_part[1], block_part[2], log_total, grad_out
        )
        grad_queries, grad_keys, grad_values = grads_from(
            queries, block_part[0], probability, grad_probs, row_delta, grad_out
        )
        return (accumulated + grad_queries, (grad_keys, grad_values))

    grad_queries, key_terms = lax.scan(grad_step, jnp.zeros(queries.shape, float_type), key_parts)
    total_keys = keys_all.shape[0]
    grad_keys = key_terms[0].reshape(total_keys, keys_all.shape[1] * keys_all.shape[2])
    grad_values = key_terms[1].reshape(total_keys, keys_all.shape[1] * keys_all.shape[2])
    return (grad_queries, grad_keys, grad_values)


def pick_block(params, block_index):
    chosen = []
    for param_array in params:
        if param_array.ndim == 2:
            chosen.append(param_array[block_index].astype(float_type))
        else:
            chosen.append(param_array[block_index])
    return tuple(chosen)


def block_forward(stream, weights, attend_fn):
    (
        first_gain,
        first_shift,
        joint_weight,
        joint_bias,
        query_gain,
        query_shift,
        key_gain,
        mixer_weight,
        mixer_bias,
        mixer_scale,
        second_gain,
        second_shift,
        inner_weight,
        inner_bias,
        outer_weight,
        outer_bias,
        outer_scale,
    ) = weights
    row_count, model_width = stream.shape
    head_count = model_width // query_gain.shape[0]
    normed = layer_norm(stream, first_gain, first_shift, norm_eps).astype(half_type)
    joined = matmul(normed, joint_weight) + joint_bias
    query_pre = split_heads(joined[:, :model_width], head_count)
    key_pre = split_heads(joined[:, model_width : 2 * model_width], head_count)
    queries = layer_norm(query_pre, query_gain, query_shift, head_eps).astype(half_type)
    key_heads = key_norm(key_pre, key_gain).astype(half_type)
    values = split_heads(joined[:, 2 * model_width :], head_count).astype(half_type)
    attended_full, context = attend_fn(queries, key_heads, values)
    attended = attended_full.reshape(row_count, model_width).astype(half_type)
    branch = matmul(attended, mixer_weight) + mixer_bias
    middle = stream + mixer_scale * branch
    normed_mid = layer_norm(middle, second_gain, second_shift, norm_eps).astype(half_type)
    hidden_pre = matmul(normed_mid, inner_weight) + inner_bias
    hidden = gelu_exact(hidden_pre).astype(half_type)
    feed_out = matmul(hidden, outer_weight) + outer_bias
    result = middle + outer_scale * feed_out
    kept = (
        stream,
        normed,
        query_pre,
        key_pre,
        queries,
        key_heads,
        values,
        context,
        attended,
        branch,
        middle,
        normed_mid,
        hidden_pre,
        hidden,
        feed_out,
    )
    return (result, kept)


def block_backward(grad_result, weights, kept, attend_back):
    (
        first_gain,
        first_shift,
        joint_weight,
        joint_bias,
        query_gain,
        query_shift,
        key_gain,
        mixer_weight,
        mixer_bias,
        mixer_scale,
        second_gain,
        second_shift,
        inner_weight,
        inner_bias,
        outer_weight,
        outer_bias,
        outer_scale,
    ) = weights
    (
        stream,
        normed,
        query_pre,
        key_pre,
        queries,
        key_heads,
        values,
        context,
        attended,
        branch,
        middle,
        normed_mid,
        hidden_pre,
        hidden,
        feed_out,
    ) = kept
    row_count, model_width = stream.shape
    head_count = model_width // query_gain.shape[0]
    grad_outer_scale = jnp.sum(grad_result * feed_out, axis=0)
    grad_feed = (grad_result * outer_scale).astype(half_type)
    grad_outer_weight = matmul_rows(hidden, grad_feed)
    grad_outer_bias = jnp.sum(grad_feed.astype(float_type), axis=0)
    grad_hidden = matmul_back(grad_feed, outer_weight)
    _, gelu_pull = jax.vjp(gelu_exact, hidden_pre)
    grad_pre = gelu_pull(grad_hidden)[0].astype(half_type)
    grad_inner_weight = matmul_rows(normed_mid, grad_pre)
    grad_inner_bias = jnp.sum(grad_pre.astype(float_type), axis=0)
    grad_normed_mid = matmul_back(grad_pre, inner_weight)
    _, second_pull = jax.vjp(
        partial(layer_norm, epsilon=norm_eps), middle, second_gain, second_shift
    )
    grad_mid_part, grad_second_gain, grad_second_shift = second_pull(grad_normed_mid)
    grad_middle = grad_result + grad_mid_part
    grad_mixer_scale = jnp.sum(grad_middle * branch, axis=0)
    grad_branch = (grad_middle * mixer_scale).astype(half_type)
    grad_mixer_weight = matmul_rows(attended, grad_branch)
    grad_mixer_bias = jnp.sum(grad_branch.astype(float_type), axis=0)
    grad_attended = matmul_back(grad_branch, mixer_weight).astype(half_type)
    grad_queries, grad_keys, grad_values = attend_back(
        queries, key_heads, values, context, split_heads(grad_attended, head_count)
    )
    _, query_pull = jax.vjp(
        partial(layer_norm, epsilon=head_eps), query_pre, query_gain, query_shift
    )
    grad_query_pre, grad_query_gain, grad_query_shift = query_pull(grad_queries)
    _, key_pull = jax.vjp(key_norm, key_pre, key_gain)
    grad_key_pre, grad_key_gain = key_pull(grad_keys)
    grad_joined = jnp.concatenate(
        [
            grad_query_pre.reshape(row_count, model_width),
            grad_key_pre.reshape(row_count, model_width),
            grad_values.reshape(row_count, model_width),
        ],
        axis=1,
    ).astype(half_type)
    grad_joint_weight = matmul_rows(normed, grad_joined)
    grad_joint_bias = jnp.sum(grad_joined.astype(float_type), axis=0)
    grad_normed = matmul_back(grad_joined, joint_weight)
    _, first_pull = jax.vjp(partial(layer_norm, epsilon=norm_eps), stream, first_gain, first_shift)
    grad_stream_part, grad_first_gain, grad_first_shift = first_pull(grad_normed)
    grad_stream = grad_middle + grad_stream_part
    grads = (
        grad_first_gain,
        grad_first_shift,
        grad_joint_weight,
        grad_joint_bias,
        grad_query_gain,
        grad_query_shift,
        grad_key_gain,
        grad_mixer_weight,
        grad_mixer_bias,
        grad_mixer_scale,
        grad_second_gain,
        grad_second_shift,
        grad_inner_weight,
        grad_inner_bias,
        grad_outer_weight,
        grad_outer_bias,
        grad_outer_scale,
    )
    return (grad_stream, grads)


def local(
    tokens,
    patch_counts,
    first_gain,
    first_shift,
    joint_weight,
    joint_bias,
    query_gain,
    query_shift,
    key_gain,
    mixer_weight,
    mixer_bias,
    mixer_scale,
    second_gain,
    second_shift,
    inner_weight,
    inner_bias,
    outer_weight,
    outer_bias,
    outer_scale,
    cotangent,
):
    params = (
        first_gain,
        first_shift,
        joint_weight,
        joint_bias,
        query_gain,
        query_shift,
        key_gain,
        mixer_weight,
        mixer_bias,
        mixer_scale,
        second_gain,
        second_shift,
        inner_weight,
        inner_bias,
        outer_weight,
        outer_bias,
        outer_scale,
    )
    row_count = tokens.shape[1]
    model_width = tokens.shape[2]
    head_count = model_width // query_gain.shape[1]
    stream_in = tokens[0].astype(float_type)
    positions = lax.iota(jnp.int32, row_count)
    valid_mask = (positions < patch_counts[0, 0] + SPECIAL).astype(float_type)
    frame_bias = (valid_mask - 1.0) * mask_depth

    def frame_attend(queries, key_heads, values):
        scores = raw_scores(queries, key_heads, frame_bias)
        log_total = jax.nn.logsumexp(scores, axis=-1, keepdims=True)
        probability = jnp.exp(scores - log_total).astype(half_type)
        attended = jnp.einsum(
            "hqk,khe->qhe", probability, values, preferred_element_type=float_type
        )
        return (attended, (log_total,))

    def frame_back(queries, key_heads, values, context, grad_out):
        probability, grad_probs = score_parts(
            queries, key_heads, values, frame_bias, context[0], grad_out
        )
        row_delta = jnp.sum(probability * grad_probs, axis=-1, keepdims=True)
        return grads_from(queries, key_heads, probability, grad_probs, row_delta, grad_out)

    def open_shared(shared):
        return (
            split_heads(shared[0], head_count),
            split_heads(shared[1], head_count),
            (shared[2].astype(float_type) - 1.0) * mask_depth,
        )

    def global_attend(queries, key_heads, values):
        shared = (
            lax.all_gather(key_heads.reshape(row_count, model_width), "frame", axis=0, tiled=True),
            lax.all_gather(values.reshape(row_count, model_width), "frame", axis=0, tiled=True),
            lax.all_gather(valid_mask.astype(half_type), "frame", axis=0, tiled=True),
        )
        keys_all, values_all, bias_all = open_shared(shared)
        key_span = block_span(keys_all.shape[0], row_count)
        attended, log_total = global_forward(queries, keys_all, values_all, bias_all, key_span)
        context = (log_total, keys_all, values_all, bias_all)
        return (attended, context)

    def global_back(queries, key_heads, values, context, grad_out):
        log_total, keys_all, values_all, bias_all = context
        key_span = block_span(keys_all.shape[0], row_count)
        grad_queries, grad_keys, grad_values = global_backward(
            queries, keys_all, values_all, bias_all, log_total, grad_out, key_span
        )
        own_keys, own_values = (
            lax.psum_scatter(grad_keys, "frame", scatter_dimension=0, tiled=True),
            lax.psum_scatter(grad_values, "frame", scatter_dimension=0, tiled=True),
        )
        return (
            grad_queries,
            split_heads(own_keys, head_count),
            split_heads(own_values, head_count),
        )

    frame_weights = pick_block(params, 0)
    global_weights = pick_block(params, 1)
    first_out, frame_kept = block_forward(stream_in, frame_weights, frame_attend)
    second_out, global_kept = block_forward(first_out, global_weights, global_attend)
    layer_out = (second_out * valid_mask[:, None]).astype(half_type)[None]
    grad_second = cotangent[0].astype(float_type) * valid_mask[:, None]
    grad_first, global_grads = block_backward(grad_second, global_weights, global_kept, global_back)
    grad_stream, frame_grads = block_backward(grad_first, frame_weights, frame_kept, frame_back)
    stacked = [
        jnp.stack([frame_part, global_part])
        for frame_part, global_part in zip(frame_grads, global_grads)
    ]
    matrix_sums = list(
        (
            lax.psum_scatter(stacked[2], ("scene", "frame"), scatter_dimension=1, tiled=True),
            lax.psum_scatter(stacked[7], ("scene", "frame"), scatter_dimension=1, tiled=True),
            lax.psum_scatter(stacked[12], ("scene", "frame"), scatter_dimension=1, tiled=True),
            lax.psum_scatter(stacked[14], ("scene", "frame"), scatter_dimension=1, tiled=True),
        )
    )
    vector_sums = list(
        lax.psum(
            (
                stacked[0],
                stacked[1],
                stacked[3],
                stacked[4],
                stacked[5],
                stacked[6],
                stacked[8],
                stacked[9],
                stacked[10],
                stacked[11],
                stacked[13],
                stacked[15],
                stacked[16],
            ),
            ("scene", "frame"),
        )
    )
    matrix_slots = (2, 7, 12, 14)
    matrix_list = list(matrix_sums)
    vector_list = list(vector_sums)
    outputs = []
    for param_slot in range(17):
        if param_slot in matrix_slots:
            outputs.append(matrix_list.pop(0))
        else:
            outputs.append(vector_list.pop(0))
    grad_tokens = grad_stream.astype(half_type)[None]
    return (layer_out, grad_tokens) + tuple(outputs)


def solution(mesh):
    in_specs = (
        P("scene", "frame", None),
        P("scene", "frame"),
        P(),
        P(),
        P(),
        P(),
        P(),
        P(),
        P(),
        P(),
        P(),
        P(),
        P(),
        P(),
        P(),
        P(),
        P(),
        P(),
        P(),
        P("scene", "frame", None),
    )
    out_specs = (
        P("scene", "frame", None),
        P("scene", "frame", None),
        P(),
        P(),
        P(None, ("scene", "frame"), None),
        P(),
        P(),
        P(),
        P(),
        P(None, ("scene", "frame"), None),
        P(),
        P(),
        P(),
        P(),
        P(None, ("scene", "frame"), None),
        P(),
        P(None, ("scene", "frame"), None),
        P(),
        P(),
    )
    return jax.shard_map(local, mesh=mesh, in_specs=in_specs, out_specs=out_specs, check_vma=False)
```

profile of v0, /device:TPU:0, one launch (start us, length us, event | category | flops | bytes accessed | tf_op | source)
XLA Modules:
  0.0 1969.3 jit_solution(13591902123582028456)
XLA Ops:
  32.6 5.0 fusion.88
  37.7 10.5 fusion.222
  68.1 36.4 %all-reduce = bf16[2304]{0:T(1024)(128)(2,1)S(1)} all-reduce(bf16[2304]{0:T(1024)(128)(2,1)S(1)} %dynamic-update-slice), channel_id=1, replica_groups=mesh['scene'=2,'frame'=16] {'frame'}, use_global_device_ids=true, to_apply=%add | all-reduce | flops 2304 | bytes 9216
  107.6 13.5 reshape.547
  121.1 12.4 copy.256
  133.5 29.0 %all-gather.5.cloned.1.call-done = bf16[2304,1024]{1,0:T(8,128)(2,1)} async-done(((bf16[144,1024]{1,0:T(8,128)(2,1)}), bf16[2304,1024]{1,0:T(8,128)(2,1)}) %all-gather.5.cloned.1.call-update) | async-done | bytes 4718608 | tf_op jit(solution)/shard_map/all_gather | solution.py:415
  162.5 13.1 reshape.548
  175.6 12.4 copy.257
  188.0 34.2 %while.50 = (s32[]{:T(128)}, f32[16,144,1]{1,0,2:T(8,128)S(1)}, f32[16,144,1]{1,0,2:T(8,128)S(1)}, bf16[4,576,16,64]{1,3,2,0:T(8,128)(2,1)}, bf16[144,16,64]{0,2...) while((s32[]{:T(128)}, f32[16,144,1]{1,0,2:T(8,128)S(1)}, ...), condition=%wide.region_19.20_spmd.clone, body=%wide.region_16.19_spmd.clone.sunk | while | flops 179170560 | bytes 12351600 | solution.py:114
  188.0 5.0 bitcast_reduce_fusion.2
  196.6 4.9 bitcast_reduce_fusion.2
  205.2 4.9 bitcast_reduce_fusion.2
  213.7 4.9 bitcast_reduce_fusion.2
  222.2 18.4 while.51
  222.3 4.5 fusion.288
  226.9 4.6 fusion.288
  231.5 4.5 fusion.288
  236.1 4.5 fusion.288
  244.2 5.0 fusion.91
  249.3 11.8 convert_reduce_fusion.1
  268.5 23.1 %while.52 = (s32[]{:T(128)}, f32[16,144,1]{1,2,0:T(1,128)S(1)}, bf16[4,576,16,64]{1,3,2,0:T(8,128)(2,1)}, bf16[144,16,64]{0,2,1:T(8,128)(2,1)S(1)}, f32[4,576]{1...) while((s32[]{:T(128)}, f32[16,144,1]{1,2,0:T(1,128)S(1)}, ...), condition=%wide.region_28.29_spmd.clone, body=%wide.region_26.28_spmd.clone.sunk | while | flops 346376448 | bytes 13881219 | solution.py:141
  291.5 76.6 %while.53 = (s32[]{:T(128)}, f32[144,16,64]{0,2,1:T(8,128)}, f32[4,576,16,64]{1,3,2,0:T(8,128)}, f32[4,576,16,64]{1,3,2,0:T(8,128)}, bf16[4,576,16,64]{1,3,2,0:T...) while((s32[]{:T(128)}, f32[144,16,64]{0,2,1:T(8,128)}, ...), condition=%wide.region_30.31_spmd.clone, body=%wide.region_29.30_spmd.clone.sunk | while | flops 863649792 | bytes 81203464 | solution.py:162
  294.3 5.0 multiply_convert_fusion.22
  313.1 5.0 multiply_convert_fusion.22
  332.3 5.0 multiply_convert_fusion.22
  344.8 4.2 bitcast_dynamic-update-slice_fusion.5
  351.5 5.0 multiply_convert_fusion.22
  368.1 15.2 copy.292
  383.3 16.6 reshape.545
  400.0 15.7 copy.293
  415.7 17.3 reshape.546
  447.7 62.3 %reduce-scatter.7.cloned.1.call-done = f32[144,1024]{1,0:T(8,128)} async-done(((f32[2304,1024]{1,0:T(8,128)}), f32[144,1024]{1,0:T(8,128)}) %reduce-scatter.7.cloned.1.call-update) | async-done | bytes 589840 | tf_op jit(solution)/shard_map/reduce_scatter | solution.py:432
  517.1 108.5 %reduce-scatter.9.cloned.1.call-done = f32[144,1024]{1,0:T(8,128)} async-done(((f32[2304,1024]{1,0:T(8,128)}), f32[144,1024]{1,0:T(8,128)}) %reduce-scatter.9.cloned.1.call-update) | async-done | bytes 589840 | tf_op jit(solution)/shard_map/reduce_scatter | solution.py:433
  629.3 5.9 multiply_reduce_fusion.16
  635.8 11.1 fusion.169
  647.7 8.8 convert_reduce_fusion.2
  656.5 7.5 multiply_reduce_fusion.12
  697.1 8.5 pad_maximum_fusion.3
  711.4 8.6 pad_maximum_fusion.2
  727.6 11.4 pad_maximum_fusion
  740.0 8.7 convolution_bitcast_fusion
  748.7 8.6 convolution_bitcast_fusion.1
  757.3 11.4 pad_maximum_fusion.1
  770.9 56.6 %all-reduce.4.cloned.1.call-done = (f32[2,1024]{1,0:T(2,128)}, f32[2,1024]{1,0:T(2,128)}, f32[2,3072]{1,0:T(2,128)}, f32[2,64]{1,0:T(2,128)}, f32[2,64]{1,0:T(2,...) async-done(((f32[2,1024]{1,0:T(2,128)}, f32[2,1024]{1,0:T(2,128)}, ...) | async-done | bytes 124432 | tf_op jit(solution)/shard_map/psum | solution.py:462
  827.5 151.2 %reduce-scatter.13.cloned.1.call-done = f32[2,32,1024]{2,1,0:T(8,128)} async-done(((f32[2,1024,1024]{2,1,0:T(8,128)}), f32[2,32,1024]{2,1,0:T(8,128)}) %reduce-scatter.13.cloned.1.call-update) | async-done | bytes 262160 | tf_op jit(solution)/shard_map/reduce_scatter | solution.py:456
  978.6 249.9 %reduce-scatter.11.cloned.1.call-done = f32[2,32,3072]{2,1,0:T(8,128)} async-done(((f32[2,1024,3072]{2,1,0:T(8,128)}), f32[2,32,3072]{2,1,0:T(8,128)}) %reduce-scatter.11.cloned.1.call-update) | async-done | bytes 786448 | tf_op jit(solution)/shard_map/reduce_scatter | solution.py:455
  1228.6 356.6 %reduce-scatter.15.cloned.1.call-done = f32[2,32,4096]{2,1,0:T(8,128)} async-done(((f32[2,1024,4096]{2,1,0:T(8,128)}), f32[2,32,4096]{2,1,0:T(8,128)}) %reduce-scatter.15.cloned.1.call-update) | async-done | bytes 1048592 | tf_op jit(solution)/shard_map/reduce_scatter | solution.py:457
  1585.2 360.5 %reduce-scatter.17.cloned.1.call-done = f32[2,128,1024]{2,1,0:T(8,128)} async-done(((f32[2,4096,1024]{2,1,0:T(8,128)}), f32[2,128,1024]{2,1,0:T(8,128)}) %reduce-scatter.17.cloned.1.call-update) | async-done | bytes 1048592 | tf_op jit(solution)/shard_map/reduce_scatter | solution.py:458
  (746 shorter events, 238.2 us)
Async XLA Ops:
  7.2 100.4 %all-gather.3.cloned.1.call-start = ((), (), s32[]{:S(2)}) async-start(), calls=%async_computation.6 | async-start | bytes 5013504 | tf_op jit(solution)/shard_map/all_gather | solution.py:416
  9.4 39.0 %copy-start.110 = (f32[1,1024]{1,0:T(1,128)}, f32[1,1024]{1,0:T(1,128)S(1)}, u32[]{:S(2)}) copy-start(f32[1,1024]{1,0:T(1,128)S(1)} %get-tuple-element.647) | copy-start | bytes 12292
  10.2 38.3 %copy-start.103 = (f32[1,1024]{1,0:T(1,128)}, f32[1,1024]{1,0:T(1,128)S(1)}, u32[]{:S(2)}) copy-start(f32[1,1024]{1,0:T(1,128)S(1)} %get-tuple-element.645) | copy-start | bytes 12292
  30.1 214.0 %copy-start.108 = (f32[1,1024]{1,0:T(1,128)}, f32[1,1024]{1,0:T(1,128)S(1)}, u32[]{:S(2)}) copy-start(f32[1,1024]{1,0:T(1,128)S(1)} %get-tuple-element.637) | copy-start | bytes 12292
  30.1 234.6 %copy-start.93 = (f32[1,1024]{1,0:T(1,128)}, f32[1,1024]{1,0:T(1,128)S(1)}, u32[]{:S(2)}) copy-start(f32[1,1024]{1,0:T(1,128)S(1)} %get-tuple-element.635) | copy-start | bytes 12292
  32.6 15.9 slice-start.8
  48.2 192.5 %copy-start.17 = (f32[144,1024]{1,0:T(8,128)}, f32[144,1024]{1,0:T(8,128)S(1)}, u32[]{:S(2)}) copy-start(f32[144,1024]{1,0:T(8,128)S(1)} %get-tuple-element.615) | copy-start | bytes 1769476
  50.6 111.9 %all-gather.5.cloned.1.call-start = ((), (), s32[]{:S(2)}) async-start(), calls=%async_computation.7 | async-start | bytes 5013504 | tf_op jit(solution)/shard_map/all_gather | solution.py:415
  63.3 446.8 %reduce-scatter.7.cloned.1.call-start = ((), (), s32[]{:S(2)}) async-start(), calls=%async_computation.8 | async-start | bytes 10027008 | tf_op jit(solution)/shard_map/reduce_scatter | solution.py:432
  64.3 56.8 %copy-start.38 = (f32[144,16]{1,0:T(8,128)}, f32[144,16]{1,0:T(8,128)S(1)}, u32[]{:S(2)}) copy-start(f32[144,16]{1,0:T(8,128)S(1)} %copy.251) | copy-start | bytes 27652
  65.1 56.0 %copy-start.101 = (f32[144,16]{0,1:T(8,128)}, f32[144,16]{0,1:T(8,128)S(1)}, u32[]{:S(2)}) copy-start(f32[144,16]{0,1:T(8,128)S(1)} %copy.252) | copy-start | bytes 27652
  65.2 55.9 %copy-start.57 = (f32[144,16]{1,0:T(8,128)}, f32[144,16]{1,0:T(8,128)S(1)}, u32[]{:S(2)}) copy-start(f32[144,16]{1,0:T(8,128)S(1)} %copy.253) | copy-start | bytes 27652
  104.5 160.5 %copy-start.201 = (f32[144]{0:T(256)}, f32[144]{0:T(256)S(1)}, u32[]{:S(2)}) copy-start(f32[144]{0:T(256)S(1)} %compare_convert_fusion) | copy-start | bytes 1732
  188.0 34.2 %copy-start.66 = (f32[144,16,64]{0,2,1:T(8,128)S(1)}, f32[144,16,64]{0,2,1:T(8,128)}, u32[]{:S(2)}) copy-start(f32[144,16,64]{0,2,1:T(8,128)} %custom-call.2) | copy-start | bytes 1769476
  222.2 18.5 copy-start.120
  222.2 18.5 copy-start.143
  243.9 20.8 %copy-start.15 = (f32[144,1024]{1,0:T(8,128)}, f32[144,1024]{1,0:T(8,128)S(1)}, u32[]{:S(2)}) copy-start(f32[144,1024]{1,0:T(8,128)S(1)} %get-tuple-element.613) | copy-start | bytes 1769476
  243.9 20.8 %copy-start.129 = (f32[144]{0:T(256)}, f32[144]{0:T(256)S(1)}, u32[]{:S(2)}) copy-start(f32[144]{0:T(256)S(1)} %broadcast_multiply_fusion.4) | copy-start | bytes 1732
  244.1 20.6 %copy-start.137 = (f32[144]{0:T(256)}, f32[144]{0:T(256)S(1)}, u32[]{:S(2)}) copy-start(f32[144]{0:T(256)S(1)} %fusion.206) | copy-start | bytes 1732
  244.2 16.9 slice-start.4
  249.2 11.9 copy-start.208
  249.2 11.8 slice-start.5
  399.9 225.7 %reduce-scatter.9.cloned.1.call-start = ((), (), s32[]{:S(2)}) async-start(), calls=%async_computation.9 | async-start | bytes 10027008 | tf_op jit(solution)/shard_map/reduce_scatter | solution.py:433
  433.0 394.5 %all-reduce.4.cloned.1.call-start = ((), (), s32[]{:S(2)}) async-start(), calls=%async_computation.14 | async-start | bytes 251904 | tf_op jit(solution)/shard_map/psum | solution.py:462
  445.0 66.3 %copy-start.14 = (f32[144,16,64]{2,1,0:T(8,128)S(1)}, f32[144,16,64]{2,1,0:T(8,128)}, u32[]{:S(2)}) copy-start(f32[144,16,64]{2,1,0:T(8,128)} %copy-done.13) | copy-start | bytes 1769476
  445.0 66.3 %copy-start.53 = (f32[144,16]{1,0:T(8,128)S(1)}, f32[144,16]{1,0:T(8,128)}, u32[]{:S(2)}) copy-start(f32[144,16]{1,0:T(8,128)} %copy-done.52) | copy-start | bytes 27652
  445.1 66.3 %copy-start.168 = (f32[64]{0:T(128)S(1)}, f32[64]{0:T(128)}, u32[]{:S(2)}) copy-start(f32[64]{0:T(128)} %get-tuple-element.653) | copy-start | bytes 772
  447.7 64.5 %copy-start.100 = (f32[144,16]{0,1:T(8,128)S(1)}, f32[144,16]{0,1:T(8,128)}, u32[]{:S(2)}) copy-start(f32[144,16]{0,1:T(8,128)} %copy-done.99) | copy-start | bytes 27652
  447.7 64.6 %copy-start.72 = (f32[144,16]{1,0:T(8,128)S(1)}, f32[144,16]{1,0:T(8,128)}, u32[]{:S(2)}) copy-start(f32[144,16]{1,0:T(8,128)} %copy-done.71) | copy-start | bytes 27652
  515.6 111.2 %copy-start.27 = (f32[144,1024]{1,0:T(8,128)S(1)}, f32[144,1024]{1,0:T(8,128)}, u32[]{:S(2)}) copy-start(f32[144,1024]{1,0:T(8,128)} %copy-done.26) | copy-start | bytes 1769476
  515.6 111.2 %copy-start.29 = (f32[144,1024]{1,0:T(8,128)S(1)}, f32[144,1024]{1,0:T(8,128)}, u32[]{:S(2)}) copy-start(f32[144,1024]{1,0:T(8,128)} %copy-done.28) | copy-start | bytes 1769476
  515.6 111.2 %copy-start.49 = (f32[144,1024]{1,0:T(8,128)S(1)}, f32[144,1024]{1,0:T(8,128)}, u32[]{:S(2)}) copy-start(f32[144,1024]{1,0:T(8,128)} %reduce-scatter.7.cloned.1.call-done) | copy-start | bytes 1769476
  515.6 111.2 %copy-start.122 = (f32[1024]{0:T(1024)S(1)}, f32[1024]{0:T(1024)}, u32[]{:S(2)}) copy-start(f32[1024]{0:T(1024)} %copy-done.121) | copy-start | bytes 12292
  517.1 112.1 %copy-start.18 = (f32[144,1024]{1,0:T(8,128)S(1)}, f32[144,1024]{1,0:T(8,128)}, u32[]{:S(2)}) copy-start(f32[144,1024]{1,0:T(8,128)} %copy-done.17) | copy-start | bytes 1769476
  517.1 112.1 %copy-start.40 = (bf16[144,1024]{1,0:T(8,128)(2,1)S(1)}, bf16[144,1024]{1,0:T(8,128)(2,1)}, u32[]{:S(2)}) copy-start(bf16[144,1024]{1,0:T(8,128)(2,1)} %reshape.497) | copy-start | bytes 884740
  517.1 112.1 %copy-start.104 = (f32[1,1024]{1,0:T(1,128)S(1)}, f32[1,1024]{1,0:T(1,128)}, u32[]{:S(2)}) copy-start(f32[1,1024]{1,0:T(1,128)} %copy-done.103) | copy-start | bytes 12292
  517.1 112.1 %copy-start.127 = (f32[144]{0:T(256)S(1)}, f32[144]{0:T(256)}, u32[]{:S(2)}) copy-start(f32[144]{0:T(256)} %copy-done.126) | copy-start | bytes 1732
  517.1 112.1 %copy-start.135 = (f32[144]{0:T(256)S(1)}, f32[144]{0:T(256)}, u32[]{:S(2)}) copy-start(f32[144]{0:T(256)} %copy-done.134) | copy-start | bytes 1732
  629.3 18.3 slice-start
  635.7 11.9 slice-start.1
  635.7 11.9 slice-start.2
  635.7 11.9 slice-start.3
  635.8 11.9 copy-start.207
  672.7 12.3 copy-start.32
  697.0 281.6 %reduce-scatter.13.cloned.1.call-start = ((), (), s32[]{:S(2)}) async-start(), calls=%async_computation.11 | async-start | bytes 8650752 | tf_op jit(solution)/shard_map/reduce_scatter | solution.py:456
  705.6 522.9 %reduce-scatter.11.cloned.1.call-start = ((), (), s32[]{:S(2)}) async-start(), calls=%async_computation.10 | async-start | bytes 25952256 | tf_op jit(solution)/shard_map/reduce_scatter | solution.py:455
  720.1 865.0 %reduce-scatter.15.cloned.1.call-start = ((), (), s32[]{:S(2)}) async-start(), calls=%async_computation.12 | async-start | bytes 34603008 | tf_op jit(solution)/shard_map/reduce_scatter | solution.py:457
  739.1 1206.5 %reduce-scatter.17.cloned.1.call-start = ((), (), s32[]{:S(2)}) async-start(), calls=%async_computation.13 | async-start | bytes 34603008 | tf_op jit(solution)/shard_map/reduce_scatter | solution.py:458
  (195 other events, 824.2 us)
Sparse Core Ops, SparseCore 0:
  50.8 56.7 all-gather.2
  110.4 52.0 all-gather.4
  400.1 109.8 reduce-scatter.6
  514.5 111.0 reduce-scatter.8
  697.2 130.2 all-reduce.3
  830.3 148.2 reduce-scatter.12
  986.8 241.7 reduce-scatter.10
  1231.4 353.6 reduce-scatter.14
  1588.0 357.5 reduce-scatter.16
where the time goes:
time: 1990 us; the launch traced here: 1970 us
  waiting for transfers between devices  1380 us (69%)
  matrix products  255 us (13%)
  local copies, waits for them, and re-layouts  177 us (9%)
  other arithmetic  104 us (5%)
  blocking collectives  36.4 us (2%)
    reduce_scatter x1, waiting for transfers between devices, local(): lax.psum_scatter(stacked[14], ('scene', 'frame'), scatter_dimension=1, ti...  360 us
    reduce_scatter x1, waiting for transfers between devices, local(): lax.psum_scatter(stacked[12], ('scene', 'frame'), scatter_dimension=1, ti...  357 us
    reduce_scatter x1, waiting for transfers between devices, local(): lax.psum_scatter(stacked[2], ('scene', 'frame'), scatter_dimension=1, til...  250 us
    reduce_scatter x1, waiting for transfers between devices, local(): lax.psum_scatter(stacked[7], ('scene', 'frame'), scatter_dimension=1, til...  151 us
    reduce_scatter x1, waiting for transfers between devices, global_back(): lax.psum_scatter(grad_values, 'frame', scatter_dimension=0, tiled=True)  109 us
    reduce_scatter x1, waiting for transfers between devices, global_back(): lax.psum_scatter(grad_keys, 'frame', scatter_dimension=0, tiled=True)  62.3 us
    unnamed x457, local copies, waits for them, and re-layouts  57 us
    psum x1, waiting for transfers between devices, local(): lax.psum((stacked[0], stacked[1], stacked[3], stacked[4], stacked[5], sta...  56.6 us
  transfers between devices with their start and end apart: 9, of which 9 were waited for; matrix products, arithmetic and copies ran while one was open for 8% of the time, Pallas kernels for 0%

commit v1 on v0

v1 whole, which is shorter than its diff:
```python
from functools import partial

import jax
import jax.numpy as jnp
from jax import lax
from jax.experimental import pallas as pl
from jax.experimental.pallas import tpu as pltpu
from jax.sharding import PartitionSpec as P

SPECIAL = 5
CHUNK = 512
LANES = 128
SLAB = 256
norm_eps = 1e-06
head_eps = 1e-05
closed_score = -10000.0
f32 = jnp.float32
bf16 = jnp.bfloat16


def nn(a, b):
    return lax.dot_general(a, b, (((1,), (0,)), ((), ())), preferred_element_type=f32)


def nt(a, b):
    return lax.dot_general(a, b, (((1,), (1,)), ((), ())), preferred_element_type=f32)


def tn(a, b):
    return lax.dot_general(a, b, (((0,), (0,)), ((), ())), preferred_element_type=f32)


def row(ref, index):
    return ref[...].astype(f32)[index : index + 1, :]


def col_sum(value):
    return jnp.sum(value, axis=0, keepdims=True)


def center_norm(value, eps):
    centered = value - jnp.mean(value, axis=-1, keepdims=True)
    spread = lax.rsqrt(jnp.mean(centered * centered, axis=-1, keepdims=True) + eps)
    return centered * spread, spread


def norm_back(grad_hat, hat, spread):
    mean_grad = jnp.mean(grad_hat, axis=-1, keepdims=True)
    mean_both = jnp.mean(grad_hat * hat, axis=-1, keepdims=True)
    return spread * (grad_hat - mean_grad - hat * mean_both)


def seg_matrix(width, head, value):
    shift = head.bit_length() - 1
    first = lax.shift_right_logical(lax.broadcasted_iota(jnp.int32, (width, width), 0), shift)
    second = lax.shift_right_logical(lax.broadcasted_iota(jnp.int32, (width, width), 1), shift)
    return jnp.where(first == second, value, 0.0).astype(bf16)


def seg_dot(value, matrix):
    high = value.astype(bf16)
    low = (value - high.astype(f32)).astype(bf16)
    return nn(high, matrix) + nn(low, matrix)


def seg_norm(value, mean_matrix):
    centered = value - seg_dot(value, mean_matrix)
    spread = lax.rsqrt(seg_dot(centered * centered, mean_matrix) + head_eps)
    return centered * spread, spread


def first_lanes(rows):
    return lax.broadcasted_iota(jnp.int32, (rows, LANES), 1) < LANES // 2


def turn(value):
    return pltpu.roll(value, LANES // 2, value.ndim - 1)


def pack_pair(slab):
    half = slab.shape[0] // 2
    top, bottom = slab[:half], slab[half:]
    low = first_lanes(half)
    return jnp.where(low, top, turn(bottom)), jnp.where(low, turn(top), bottom)


def unpack_pair(even, odd):
    low = first_lanes(even.shape[0])
    top = jnp.where(low, even, turn(odd))
    bottom = jnp.where(low, turn(even), odd)
    return jnp.concatenate([top, bottom], axis=0)


def erf(value):
    value = jnp.clip(value, -4.0, 4.0)
    square = value * value
    top = jnp.full_like(square, -2.72614225801306e-10)
    for coefficient in (
        2.77068142495902e-08,
        -2.10102402082508e-06,
        -5.69250639462346e-05,
        -7.34990630326855e-04,
        -2.95459980854025e-03,
        -1.60960333262415e-02,
    ):
        top = top * square + coefficient
    bottom = jnp.full_like(square, -1.45660718464996e-05)
    for coefficient in (
        -2.13374055278905e-04,
        -1.68282697438203e-03,
        -7.37332916720468e-03,
        -1.42647390514189e-02,
    ):
        bottom = bottom * square + coefficient
    return value * top / bottom


def full(shape):
    return pl.BlockSpec(shape, lambda *_: (0,) * len(shape))


def sds(shape, dtype):
    return jax.ShapeDtypeStruct(shape, dtype)


def call(body, name, grid, in_specs, out_specs, out_shape, scratch, flops, moved):
    return pl.pallas_call(
        body,
        name=name,
        out_shape=out_shape,
        grid_spec=pltpu.PrefetchScalarGridSpec(
            num_scalar_prefetch=1,
            grid=grid,
            in_specs=in_specs,
            out_specs=out_specs,
            scratch_shapes=scratch,
        ),
        cost_estimate=pl.CostEstimate(flops=flops, bytes_accessed=moved, transcendentals=0),
    )


def joint_body(
    block, packed, head, meta, x_ref, gain_ref, shift_ref, pattern_ref, w_ref, b_ref,
    own_ref, other_ref, pre_ref, out_ref, normed_ref, *stage
):
    step = pl.program_id(0)
    rows, width = normed_ref.shape
    per_part = width // CHUNK
    half = rows // 2

    @pl.when(step == 0)
    def _():
        hat, _ = center_norm(x_ref[...].astype(f32), norm_eps)
        normed = (hat * row(gain_ref, block) + row(shift_ref, block)).astype(bf16)
        normed_ref[...] = normed

        @pl.when(meta[0] == 0)
        def _():
            own_ref[...] = normed[:, : width // 2]
            other_ref[...] = normed[:, width // 2 :]

        @pl.when(meta[0] != 0)
        def _():
            own_ref[...] = normed[:, width // 2 :]
            other_ref[...] = normed[:, : width // 2]

        if packed:
            count = jnp.full((8, LANES), meta[3], jnp.int32).astype(f32)
            for place in range(stage[0].shape[0]):
                stage[0][place, 3 * half : 3 * half + 8, :] = count

    joined = nn(normed_ref[...], w_ref[0]) + row(b_ref, block)
    pattern = pattern_ref[...]

    def emit(part, values):
        if packed:
            base = (step - part * per_part) * (CHUNK // head)
            for slab in range(CHUNK // LANES):
                even, odd = pack_pair(values[:, slab * LANES : (slab + 1) * LANES])
                stage[0][base + 2 * slab, part * half : (part + 1) * half, :] = even
                stage[0][base + 2 * slab + 1, part * half : (part + 1) * half, :] = odd
        else:
            out_ref[...] = values.astype(bf16)

    def normed_heads(gain, shift):
        mean_matrix = seg_matrix(SLAB, head, 1.0 / head)
        pieces = []
        for slab in range(CHUNK // SLAB):
            hat, _ = seg_norm(joined[:, slab * SLAB : (slab + 1) * SLAB], mean_matrix)
            pieces.append(hat * gain if shift is None else hat * gain + shift)
        return jnp.concatenate(pieces, axis=1)

    scale = head ** (-0.5)

    @pl.when(step < per_part)
    def _():
        pre_ref[...] = joined
        emit(0, normed_heads(
            pattern[3 * block : 3 * block + 1] * scale,
            pattern[3 * block + 1 : 3 * block + 2] * scale,
        ))

    @pl.when((step >= per_part) & (step < 2 * per_part))
    def _():
        pre_ref[...] = joined
        emit(1, normed_heads(pattern[3 * block + 2 : 3 * block + 3], None))

    @pl.when(step >= 2 * per_part)
    def _():
        emit(2, joined)

    if packed:

        @pl.when(step == 3 * per_part - 1)
        def _():
            out_ref[...] = stage[0][...].astype(bf16)


def joint_forward(block, packed, head, meta, x, gain, shift, pattern, weight, bias):
    rows, width = x.shape
    per_part = width // CHUNK
    heads = width // head
    packed_rows = 3 * (rows // 2) + 8
    if packed:
        out_spec, out = full((heads, packed_rows, LANES)), sds((heads, packed_rows, LANES), bf16)
        extra = [pltpu.VMEM((heads, packed_rows, LANES), f32)]
    else:
        out_spec = pl.BlockSpec((rows, CHUNK), lambda j, m: (0, j))
        out = sds((rows, 3 * width), bf16)
        extra = []
    return call(
        partial(joint_body, block, packed, head),
        f"joint_forward_{block}",
        (3 * per_part,),
        [
            full((rows, width)),
            full(gain.shape),
            full(shift.shape),
            full(pattern.shape),
            pl.BlockSpec((1, width, CHUNK), lambda j, m: (block, 0, j)),
            pl.BlockSpec((2, CHUNK), lambda j, m: (0, j)),
        ],
        [
            full((rows, width // 2)),
            full((rows, width // 2)),
            pl.BlockSpec((rows, CHUNK), lambda j, m: (0, jnp.minimum(j, 2 * per_part - 1))),
            out_spec,
        ],
        [
            sds((rows, width // 2), bf16),
            sds((rows, width // 2), bf16),
            sds((rows, 2 * width), f32),
            out,
        ],
        [pltpu.VMEM((rows, width), bf16)] + extra,
        2 * rows * width * 3 * width,
        6 * width * width + 16 * rows * width,
    )(meta, x, gain, shift, pattern, weight, bias)


def lane_picks():
    lane = lax.broadcasted_iota(jnp.int32, (1, LANES), 1)
    low = jnp.where(lane < LANES // 2, 1.0, 0.0)
    return low.astype(bf16), (1.0 - low).astype(bf16)


def open_row(meta, rows):
    place = lax.broadcasted_iota(jnp.int32, (1, rows), 1)
    return jnp.where(place < meta[3] + SPECIAL, 0.0, closed_score)


def frame_body(meta, qkv_ref, out_ref):
    rows, width = out_ref.shape
    bias = open_row(meta, rows)
    picks = lane_picks()
    low = first_lanes(rows)
    for slab in range(width // LANES):
        at = slab * LANES
        queries = qkv_ref[:, at : at + LANES]
        keys = qkv_ref[:, width + at : width + at + LANES]
        values = qkv_ref[:, 2 * width + at : 2 * width + at + LANES]
        results = []
        for pick in picks:
            power = jnp.exp(nt(queries * pick, keys) + bias)
            probs = power / jnp.sum(power, axis=-1, keepdims=True)
            results.append(nn(probs.astype(bf16), values))
        out_ref[:, at : at + LANES] = jnp.where(low, results[0], results[1]).astype(bf16)


def frame_forward(meta, qkv):
    rows = qkv.shape[0]
    width = qkv.shape[1] // 3
    return call(
        frame_body,
        "frame_forward",
        (1,),
        [full(qkv.shape)],
        full((rows, width)),
        sds((rows, width), bf16),
        [],
        4 * rows * rows * width,
        8 * rows * width,
    )(meta, qkv)


def frame_back_body(meta, qkv_ref, grad_ref, out_ref):
    rows, width = grad_ref.shape
    bias = open_row(meta, rows)
    picks = lane_picks()
    low = first_lanes(rows)
    scale = (LANES // 2) ** (-0.5)
    for slab in range(width // LANES):
        at = slab * LANES
        queries = qkv_ref[:, at : at + LANES]
        keys = qkv_ref[:, width + at : width + at + LANES]
        values = qkv_ref[:, 2 * width + at : 2 * width + at + LANES]
        grads = grad_ref[:, at : at + LANES]
        found = []
        for pick in picks:
            power = jnp.exp(nt(queries * pick, keys) + bias)
            probs = power / jnp.sum(power, axis=-1, keepdims=True)
            grad_probs = nt(grads * pick, values)
            delta = jnp.sum(probs * grad_probs, axis=-1, keepdims=True)
            grad_scores = (probs * (grad_probs - delta)).astype(bf16)
            found.append((
                nn(grad_scores, keys) * scale,
                tn(grad_scores, queries),
                tn(probs.astype(bf16), grads),
            ))
        for part in range(3):
            out_ref[:, part * width + at : part * width + at + LANES] = jnp.where(
                low, found[0][part], found[1][part]
            )


def frame_backward(meta, qkv, grad):
    rows, width = grad.shape
    return call(
        frame_back_body,
        "frame_backward",
        (1,),
        [full(qkv.shape), full(grad.shape)],
        full((rows, 3 * width)),
        sds((rows, 3 * width), f32),
        [],
        10 * rows * rows * width,
        20 * rows * width,
    )(meta, qkv, grad)


def packed_part(ref, part, half):
    whole = ref[...].astype(f32)
    return whole[:, part * half : (part + 1) * half, :].reshape(-1, LANES)


def open_slots(ref, half):
    count = ref[...].astype(f32)[:, 3 * half : 3 * half + 8, :]
    count = jnp.concatenate([count] * (half // 8), axis=1)
    place = lax.broadcasted_iota(jnp.int32, count.shape, 1).astype(f32)
    return (
        (place < count + SPECIAL).reshape(-1, LANES),
        (place + half < count + SPECIAL).reshape(-1, LANES),
    )


def scene_body(half, span, meta, q_ref, kv_ref, att_ref, out_ref, log_ref, queries, keys, values):
    n = queries.shape[0] // 2
    m = keys.shape[0] // 2
    q = packed_part(q_ref, 0, half)
    low_n, low_m = first_lanes(n), first_lanes(m)
    queries[:n, :] = jnp.where(low_n, q, 0.0).astype(bf16)
    queries[n:, :] = jnp.where(low_n, turn(q), 0.0).astype(bf16)
    k = packed_part(kv_ref, 1, half)
    keys[:m, :] = k.astype(bf16)
    keys[m:, :] = turn(k).astype(bf16)
    v = packed_part(kv_ref, 2, half)
    open_low, open_high = open_slots(kv_ref, half)
    values[:m, :] = jnp.where(open_low, jnp.where(low_m, v, 1.0), 0.0).astype(bf16)
    values[m:, :] = jnp.where(open_high, jnp.where(low_m, turn(v), 1.0), 0.0).astype(bf16)
    low = first_lanes(LANES)

    @pl.loop(0, n // LANES)
    def _(piece):
        at = pl.multiple_of(piece * LANES, LANES)
        some = jnp.concatenate([queries[pl.ds(at, LANES), :], queries[pl.ds(n + at, LANES), :]], axis=0)
        total = jnp.zeros((2 * LANES, LANES), f32)
        for start in range(0, 2 * m, span):
            power = jnp.exp(nt(some, keys[start : start + span, :])).astype(bf16)
            total = total + nn(power, values[start : start + span, :])
        first, second = total[:LANES], total[LANES:]
        bottom = jnp.where(low, turn(first), second)
        result = jnp.where(low, first, turn(second)) / bottom
        att_ref[pl.ds(at, LANES), :] = result.astype(bf16)
        out_ref[pl.ds(at, LANES), :] = result
        log_ref[pl.ds(at, LANES), :] = jnp.log(bottom)


def scene_forward(meta, q_pack, kv_pack, half):
    n = q_pack.shape[0] * half
    m = kv_pack.shape[0] * half
    span = m // 2
    while span > 640:
        span = span // 2
    return call(
        partial(scene_body, half, span),
        "scene_forward",
        (1,),
        [full(q_pack.shape), full(kv_pack.shape)],
        [full((n, LANES))] * 3,
        [sds((n, LANES), bf16), sds((n, LANES), f32), sds((n, LANES), f32)],
        [
            pltpu.VMEM((2 * n, LANES), bf16),
            pltpu.VMEM((2 * m, LANES), bf16),
            pltpu.VMEM((2 * m, LANES), bf16),
        ],
        4 * 4 * n * m * LANES,
        20 * n * LANES,
    )(meta, q_pack, kv_pack)


def three_lanes(value, closed):
    lane = lax.broadcasted_iota(jnp.int32, value.shape, 1)
    base = LANES // 2
    high = value.astype(bf16).astype(f32)
    rest = value - high
    middle = rest.astype(bf16).astype(f32)
    last = rest - middle
    result = jnp.where(lane == base, high, jnp.where(lane == base + 1, middle, last))
    return jnp.where(lane < base + 3, result, jnp.where(lane == base + 3, closed, 0.0))


def scene_back_body(
    half, span, meta, q_ref, kv_ref, grad_ref, out_ref, log_ref,
    dq_ref, dk_ref, dv_ref, queries, keys, values, grads, turned
):
    n = queries.shape[0] // 2
    m = keys.shape[0] // 2
    low_n, low_m = first_lanes(n), first_lanes(m)
    base = LANES // 2
    q = packed_part(q_ref, 0, half)
    log = -log_ref[...]
    queries[:n, :] = jnp.where(low_n, q, three_lanes(turn(log), closed_score)).astype(bf16)
    queries[n:, :] = jnp.where(low_n, turn(q), three_lanes(log, closed_score)).astype(bf16)
    g = grad_ref[...].astype(f32)
    delta = -seg_dot(g * out_ref[...], seg_matrix(LANES, base, 1.0))
    grads[:n, :] = jnp.where(low_n, g, three_lanes(turn(delta), 0.0)).astype(bf16)
    grads[n:, :] = jnp.where(low_n, turn(g), three_lanes(delta, 0.0)).astype(bf16)
    lane = lax.broadcasted_iota(jnp.int32, (m, LANES), 1)
    ones = jnp.where(lane < base + 3, 1.0, 0.0)
    open_low, open_high = open_slots(kv_ref, half)
    k = packed_part(kv_ref, 1, half)
    for place, k_now, is_open in ((0, k, open_low), (m, turn(k), open_high)):
        tail = jnp.where((lane == base + 3) & jnp.logical_not(is_open), 1.0, ones)
        keys[place : place + m, :] = jnp.where(low_m, k_now, tail).astype(bf16)
    v = packed_part(kv_ref, 2, half)
    values[:m, :] = jnp.where(low_m, v, ones).astype(bf16)
    values[m:, :] = jnp.where(low_m, turn(v), ones).astype(bf16)
    turned[...] = jnp.zeros_like(turned)
    low = first_lanes(LANES)

    @pl.loop(0, m // LANES)
    def _(piece):
        at = pl.multiple_of(piece * LANES, LANES)
        key_part = jnp.concatenate([keys[pl.ds(at, LANES), :], keys[pl.ds(m + at, LANES), :]], axis=0)
        value_part = jnp.concatenate(
            [values[pl.ds(at, LANES), :], values[pl.ds(m + at, LANES), :]], axis=0
        )
        key_turned = jnp.transpose(key_part.astype(f32)).astype(bf16)
        dk = jnp.zeros((2 * LANES, LANES), f32)
        dv = jnp.zeros((2 * LANES, LANES), f32)
        for start in range(0, 2 * n, span):
            some = queries[start : start + span, :]
            some_grads = grads[start : start + span, :]
            probs = jnp.exp(nt(key_part, some))
            grad_scores = (probs * nt(value_part, some_grads)).astype(bf16)
            dv = dv + nn(probs.astype(bf16), some_grads)
            dk = dk + nn(grad_scores, some)
            turned[:, start : start + span] += nn(key_turned, grad_scores)
        dk_ref[pl.ds(at, LANES), :] = jnp.where(low, dk[:LANES], turn(dk[LANES:])).astype(bf16)
        dv_ref[pl.ds(at, LANES), :] = jnp.where(low, dv[:LANES], turn(dv[LANES:])).astype(bf16)

    scale = base ** (-0.5)
    for at in range(0, n, LANES):
        first = jnp.transpose(turned[:, at : at + LANES])
        second = jnp.transpose(turned[:, n + at : n + at + LANES])
        dq_ref[at : at + LANES, :] = (jnp.where(low, first, turn(second)) * scale).astype(bf16)


def scene_backward(meta, q_pack, kv_pack, grad, out, log, half):
    n = q_pack.shape[0] * half
    m = kv_pack.shape[0] * half
    span = n // 2
    while span > 640:
        span = span // 2
    return call(
        partial(scene_back_body, half, span),
        "scene_backward",
        (1,),
        [full(q_pack.shape), full(kv_pack.shape)] + [full((n, LANES))] * 3,
        [full((n, LANES)), full((m, LANES)), full((m, LANES))],
        [sds((n, LANES), bf16), sds((m, LANES), bf16), sds((m, LANES), bf16)],
        [
            pltpu.VMEM((2 * n, LANES), bf16),
            pltpu.VMEM((2 * m, LANES), bf16),
            pltpu.VMEM((2 * m, LANES), bf16),
            pltpu.VMEM((2 * n, LANES), bf16),
            pltpu.VMEM((LANES, 2 * n), f32),
        ],
        10 * 4 * n * m * LANES,
        30 * n * LANES,
    )(meta, q_pack, kv_pack, grad, out, log)


def feed_body(
    block, packed, meta, att_ref, x_ref, mixer_ref, mixer_bias, mixer_scale, gain_ref, shift_ref,
    inner_ref, inner_bias, outer_ref, outer_bias, outer_scale,
    own_ref, other_ref, middle_ref, branch_ref, feed_ref, slope_ref, out_ref, normed_ref, total_ref
):
    step = pl.program_id(0)
    steps = pl.num_programs(0)
    rows, width = middle_ref.shape
    hidden_half = own_ref.shape[1] - width
    half_steps = hidden_half // CHUNK
    mine = meta[0]

    def split(value, at):
        first, second = value[:, : width // 2], value[:, width // 2 :]

        @pl.when(mine == 0)
        def _():
            own_ref[:, at : at + width // 2] = first
            other_ref[:, at : at + width // 2] = second

        @pl.when(mine != 0)
        def _():
            own_ref[:, at : at + width // 2] = second
            other_ref[:, at : at + width // 2] = first

    @pl.when(step == 0)
    def _():
        if packed:
            pieces = []
            for pair in range(width // LANES):
                pieces.append(
                    unpack_pair(att_ref[2 * pair].astype(f32), att_ref[2 * pair + 1].astype(f32))
                )
            attended = jnp.concatenate(pieces, axis=1).astype(bf16)
        else:
            attended = att_ref[...]
        branch = nn(attended, mixer_ref[0]) + row(mixer_bias, block)
        middle = x_ref[...].astype(f32) + row(mixer_scale, block) * branch
        hat, _ = center_norm(middle, norm_eps)
        normed = (hat * row(gain_ref, block) + row(shift_ref, block)).astype(bf16)
        branch_ref[...] = branch
        middle_ref[...] = middle
        normed_ref[...] = normed
        split(normed, hidden_half)
        split(attended, hidden_half + width // 2)
        total_ref[...] = jnp.zeros_like(total_ref)

    pre = nn(normed_ref[...], inner_ref[0]) + row(inner_bias, block)
    share = 0.5 * (1.0 + erf(pre * (2.0 ** (-0.5))))
    slope_ref[...] = share + pre * jnp.exp(-0.5 * pre * pre) * 0.3989422804014327
    hidden = (pre * share).astype(bf16)
    place = pl.multiple_of(lax.rem(step, half_steps) * CHUNK, CHUNK)

    @pl.when(step // half_steps == mine)
    def _():
        own_ref[:, pl.ds(place, CHUNK)] = hidden

    @pl.when(step // half_steps != mine)
    def _():
        other_ref[:, pl.ds(place, CHUNK)] = hidden

    total_ref[...] += nn(hidden, outer_ref[0])

    @pl.when(step == steps - 1)
    def _():
        feed = total_ref[...] + row(outer_bias, block)
        feed_ref[...] = feed
        result = middle_ref[...] + row(outer_scale, block) * feed
        if packed:
            place = lax.broadcasted_iota(jnp.int32, result.shape, 0)
            result = jnp.where(place < meta[3] + SPECIAL, result, 0.0)
        out_ref[...] = result.astype(out_ref.dtype)


def feed_forward(block, packed, meta, att, x, mixer, mixer_bias, mixer_scale, gain, shift, inner, inner_bias, outer, outer_bias, outer_scale):
    rows, width = x.shape
    hidden = inner.shape[2]
    kept = hidden // 2 + width
    steps = hidden // CHUNK
    vector = full(gain.shape)
    return call(
        partial(feed_body, block, packed),
        f"feed_forward_{block}",
        (steps,),
        [
            full(att.shape),
            full((rows, width)),
            pl.BlockSpec((1, width, width), lambda j, m: (block, 0, 0)),
            vector, vector, vector, vector,
            pl.BlockSpec((1, width, CHUNK), lambda j, m: (block, 0, j)),
            pl.BlockSpec((2, CHUNK), lambda j, m: (0, j)),
            pl.BlockSpec((1, CHUNK, width), lambda j, m: (block, j, 0)),
            vector, vector,
        ],
        [full((rows, kept))] * 2
        + [full((rows, width))] * 3
        + [pl.BlockSpec((rows, CHUNK), lambda j, m: (0, j)), full((rows, width))],
        [sds((rows, kept), bf16)] * 2
        + [sds((rows, width), f32)] * 3
        + [sds((rows, hidden), f32), sds((rows, width), bf16 if packed else f32)],
        [pltpu.VMEM((rows, width), bf16), pltpu.VMEM((rows, width), f32)],
        2 * rows * width * (2 * hidden + width),
        4 * width * hidden + 4 * rows * hidden + 30 * rows * width,
    )(meta, att, x, mixer, mixer_bias, mixer_scale, gain, shift, inner, inner_bias, outer, outer_bias, outer_scale)


def feed_back_body(
    block, packed, meta, g_ref, feed_ref, slope_ref, middle_ref, branch_ref,
    outer_scale, gain_ref, mixer_scale, outer_ref, inner_ref, mixer_ref,
    grads_ref, g_middle_ref, g_att_ref, vector_ref, g_feed_ref, total_ref, *kept
):
    step = pl.program_id(0)
    steps = pl.num_programs(0)
    rows, width = middle_ref.shape
    half_steps = steps // 2

    def incoming():
        g = g_ref[...].astype(f32)
        if packed:
            place = lax.broadcasted_iota(jnp.int32, g.shape, 0)
            g = jnp.where(place < meta[3] + SPECIAL, g, 0.0)
        return g

    @pl.when(step == 0)
    def _():
        g = incoming()
        g_feed = (g * row(outer_scale, block)).astype(bf16)
        g_feed_ref[...] = g_feed
        grads_ref[0, :, : width // 2] = g_feed[:, : width // 2]
        grads_ref[1, :, : width // 2] = g_feed[:, width // 2 :]
        vector_ref[0:1, :] = col_sum(g * feed_ref[...])
        vector_ref[1:2, :] = col_sum(g_feed.astype(f32))
        total_ref[...] = jnp.zeros_like(total_ref)

    g_pre = (nt(g_feed_ref[...], outer_ref[0]) * slope_ref[...]).astype(bf16)
    grads_ref[step // half_steps, :, pl.ds(pl.multiple_of(width + lax.rem(step, half_steps) * CHUNK, CHUNK), CHUNK)] = g_pre
    per_row = width // CHUNK
    vector_ref[pl.ds(6 + step // per_row, 1), pl.ds(pl.multiple_of(lax.rem(step, per_row) * CHUNK, CHUNK), CHUNK)] = col_sum(g_pre.astype(f32))
    total_ref[...] += nt(g_pre, inner_ref[0])

    @pl.when(step == steps - 1)
    def _():
        hat, spread = center_norm(middle_ref[...], norm_eps)
        g_nm = total_ref[...]
        vector_ref[2:3, :] = col_sum(g_nm * hat)
        vector_ref[3:4, :] = col_sum(g_nm)
        g_middle = incoming() + norm_back(g_nm * row(gain_ref, block), hat, spread)
        g_middle_ref[...] = g_middle
        vector_ref[4:5, :] = col_sum(g_middle * branch_ref[...])
        g_branch = (g_middle * row(mixer_scale, block)).astype(bf16)
        vector_ref[5:6, :] = col_sum(g_branch.astype(f32))
        grads_ref[0, :, width // 2 : width] = g_branch[:, : width // 2]
        grads_ref[1, :, width // 2 : width] = g_branch[:, width // 2 :]
        g_att = nt(g_branch, mixer_ref[0])
        if packed:
            for pair in range(width // LANES):
                even, odd = pack_pair(g_att[:, pair * LANES : (pair + 1) * LANES])
                g_att_ref[2 * pair] = even.astype(bf16)
                g_att_ref[2 * pair + 1] = odd.astype(bf16)
        else:
            g_att_ref[...] = g_att.astype(bf16)


def feed_backward(block, packed, heads, meta, g, feed, slope, middle, branch, outer_scale, gain, mixer_scale, outer, inner, mixer):
    rows, width = middle.shape
    hidden = inner.shape[2]
    steps = hidden // CHUNK
    vector = full(gain.shape)
    vector_rows = 6 + hidden // width
    att_shape = (heads, rows // 2, LANES) if packed else (rows, width)
    return call(
        partial(feed_back_body, block, packed),
        f"feed_backward_{block}",
        (steps,),
        [
            full((rows, width)),
            full((rows, width)),
            pl.BlockSpec((rows, CHUNK), lambda j, m: (0, j)),
            full((rows, width)),
            full((rows, width)),
            vector, vector, vector,
            pl.BlockSpec((1, CHUNK, width), lambda j, m: (block, j, 0)),
            pl.BlockSpec((1, width, CHUNK), lambda j, m: (block, 0, j)),
            pl.BlockSpec((1, width, width), lambda j, m: (block, 0, 0)),
        ],
        [
            full((2, rows, width + hidden // 2)),
            full((rows, width)),
            full(att_shape),
            full((vector_rows, width)),
        ],
        [
            sds((2, rows, width + hidden // 2), bf16),
            sds((rows, width), f32),
            sds(att_shape, bf16),
            sds((vector_rows, width), f32),
        ],
        [pltpu.VMEM((rows, width), bf16), pltpu.VMEM((rows, width), f32)],
        2 * rows * width * (2 * hidden + width),
        4 * width * hidden + 8 * rows * hidden + 20 * rows * width,
    )(meta, g, feed, slope, middle, branch, outer_scale, gain, mixer_scale, outer, inner, mixer)


def joint_back_body(
    block, packed, head, meta, g_ref, pre_ref, x_ref, g_middle_ref, gain_ref, pattern_ref, w_ref,
    grads_ref, out_ref, vector_ref, total_ref
):
    step = pl.program_id(0)
    steps = pl.num_programs(0)
    rows, width = total_ref.shape
    per_part = width // CHUNK
    half_steps = steps // 2

    @pl.when(step == 0)
    def _():
        total_ref[...] = jnp.zeros_like(total_ref)
        vector_ref[...] = jnp.zeros_like(vector_ref)

    if packed:
        pieces = []
        for pair in range(CHUNK // LANES):
            pieces.append(
                unpack_pair(g_ref[2 * pair, 0].astype(f32), g_ref[2 * pair + 1, 0].astype(f32))
            )
        g = jnp.concatenate(pieces, axis=1)
    else:
        g = g_ref[...]
    pattern = pattern_ref[...]

    def finish(g_joined):
        rounded = g_joined.astype(bf16)
        grads_ref[step // half_steps, :, pl.ds(pl.multiple_of(lax.rem(step, half_steps) * CHUNK, CHUNK), CHUNK)] = rounded
        vector_ref[pl.ds(2 + step // per_part, 1), pl.ds(pl.multiple_of(lax.rem(step, per_part) * CHUNK, CHUNK), CHUNK)] = col_sum(rounded.astype(f32))
        total_ref[...] += nt(rounded, w_ref[0])

    def head_back(gain, gain_row, shift_row):
        mean_matrix = seg_matrix(SLAB, head, 1.0 / head)
        pieces = []
        for slab in range(CHUNK // SLAB):
            at = slab * SLAB
            g_now = g[:, at : at + SLAB]
            hat, spread = seg_norm(pre_ref[:, at : at + SLAB], mean_matrix)
            vector_ref[gain_row : gain_row + 1, at : at + SLAB] += col_sum(g_now * hat)
            if shift_row is not None:
                vector_ref[shift_row : shift_row + 1, at : at + SLAB] += col_sum(g_now)
            grad_hat = g_now * gain
            pieces.append(
                spread
                * (
                    grad_hat
                    - seg_dot(grad_hat, mean_matrix)
                    - hat * seg_dot(grad_hat * hat, mean_matrix)
                )
            )
        finish(jnp.concatenate(pieces, axis=1))

    @pl.when(step < per_part)
    def _():
        head_back(pattern[3 * block : 3 * block + 1], 5, 6)

    @pl.when((step >= per_part) & (step < 2 * per_part))
    def _():
        head_back(pattern[3 * block + 2 : 3 * block + 3], 7, None)

    @pl.when(step >= 2 * per_part)
    def _():
        finish(g)

    @pl.when(step == steps - 1)
    def _():
        hat, spread = center_norm(x_ref[...].astype(f32), norm_eps)
        g_normed = total_ref[...]
        vector_ref[0:1, :] = col_sum(g_normed * hat)
        vector_ref[1:2, :] = col_sum(g_normed)
        result = g_middle_ref[...] + norm_back(g_normed * row(gain_ref, block), hat, spread)
        out_ref[...] = result.astype(out_ref.dtype)


def joint_backward(block, packed, head, meta, g, pre, x, g_middle, gain, pattern, weight):
    rows, width = x.shape
    per_part = width // CHUNK
    if packed:
        g_spec = pl.BlockSpec(
            (CHUNK // head, 1, rows // 2, LANES),
            lambda j, m: (lax.rem(j, per_part), j // per_part, 0, 0),
        )
    else:
        g_spec = pl.BlockSpec((rows, CHUNK), lambda j, m: (0, j))
    return call(
        partial(joint_back_body, block, packed, head),
        f"joint_backward_{block}",
        (3 * per_part,),
        [
            g_spec,
            pl.BlockSpec((rows, CHUNK), lambda j, m: (0, jnp.minimum(j, 2 * per_part - 1))),
            full((rows, width)),
            full((rows, width)),
            full(gain.shape),
            full(pattern.shape),
            pl.BlockSpec((1, width, CHUNK), lambda j, m: (block, 0, j)),
        ],
        [full((2, rows, 3 * width // 2)), full((rows, width)), full((8, width))],
        [
            sds((2, rows, 3 * width // 2), bf16),
            sds((rows, width), f32 if packed else bf16),
            sds((8, width), f32),
        ],
        [pltpu.VMEM((rows, width), f32)],
        2 * rows * width * 3 * width,
        6 * width * width + 30 * rows * width,
    )(meta, g, pre, x, g_middle, gain, pattern, weight)


def product_body(plan, chips, meta, *refs):
    lefts, rights = refs[:4], refs[4:8]
    send_ref, keep_ref, left, right = refs[8:]
    rows = lefts[0].shape[0]
    for index in range(4):
        left[index * rows : (index + 1) * rows, :] = lefts[index][...]
        right[index * rows : (index + 1) * rows, :] = rights[index][0]
    odd = meta[2] == 1
    for left_at, left_width, right_at, offset in plan:
        deep = left_width // chips
        for start in range(0, left_width, CHUNK):
            value = tn(
                left[:, left_at + start : left_at + start + CHUNK],
                right[:, right_at : right_at + CHUNK],
            ).astype(f32)
            value = value.reshape(CHUNK // (2 * deep), 2, deep, CHUNK)
            first = start // (2 * deep)
            last = first + CHUNK // (2 * deep)
            keep_ref[first:last, offset : offset + deep, :] = jnp.where(odd, value[:, 1], value[:, 0]).astype(bf16)
            send_ref[first:last, offset : offset + deep, :] = jnp.where(odd, value[:, 0], value[:, 1]).astype(bf16)


def product(name, plan, chips, meta, lefts, rights):
    rows, left_width = lefts[0].shape
    right_width = rights[0].shape[2]
    deep = sum(piece[1] // chips for piece in plan)
    shape = (chips // 2, deep, CHUNK)
    half = pl.BlockSpec((1, rows, right_width), lambda i, m: (m[1], 0, 0))
    return call(
        partial(product_body, plan, chips),
        name,
        (1,),
        [full((rows, left_width))] * 4 + [half] * 4,
        [full(shape)] * 2,
        [sds(shape, bf16)] * 2,
        [pltpu.VMEM((4 * rows, left_width), bf16), pltpu.VMEM((4 * rows, right_width), bf16)],
        2 * 4 * rows * deep * chips * CHUNK,
        8 * rows * (left_width + right_width) + 2 * chips * deep * CHUNK,
    )(meta, *lefts, *rights)


def local(scenes, frames, tokens, patch_counts, first_gain, first_shift, joint_weight, joint_bias, query_gain, query_shift, key_gain, mixer_weight, mixer_bias, mixer_scale, second_gain, second_shift, inner_weight, inner_bias, outer_weight, outer_bias, outer_scale, cotangent):
    rows, width = tokens.shape[1:]
    half = rows // 2
    head = query_gain.shape[1]
    heads = width // head
    hidden = inner_weight.shape[2]
    chips = frames // 2
    parts = frames // heads
    scene = lax.axis_index("scene")
    frame = lax.axis_index("frame")
    core = lax.rem(frame, 2)
    meta = jnp.stack([scene, core, lax.rem(frame // 2, 2), patch_counts[0, 0]]).astype(jnp.int32)
    pattern = jnp.tile(
        jnp.stack([vector[block] for block in range(2) for vector in (query_gain, query_shift, key_gain)]).astype(f32),
        (1, SLAB // head),
    )
    everyone = [("scene", "frame")]

    def swap_scene(value):
        return lax.ppermute(value, "scene", [(s, s ^ 1) for s in range(scenes)])

    def swap_frame(value, bit):
        return lax.ppermute(value, "frame", [(f, f ^ bit) for f in range(frames)])

    groups = [[part * heads + place for place in range(heads)] for part in range(parts)]

    def exchange(value):
        if parts == 1:
            return lax.all_to_all(value, "frame", 0, 0, tiled=True)
        return lax.all_to_all(value, "frame", 0, 0, tiled=True, axis_index_groups=groups)

    def to_heads(value):
        if parts > 1:
            value = jnp.tile(value, (parts, 1, 1))
        everything = lax.all_to_all(value, "frame", 0, 0, tiled=True)
        if parts == 1:
            return everything, everything
        return lax.dynamic_slice_in_dim(everything, (frame // heads) * heads, heads, 0), everything

    def from_heads(dq, dk, dv):
        if parts == 1:
            value = jnp.stack([part.reshape(heads, half, LANES) for part in (dq, dk, dv)], axis=1)
            return exchange(value)
        dq = exchange(dq.reshape(heads, half, LANES))
        both = jnp.stack([part.reshape(frames, half, LANES) for part in (dk, dv)], axis=1)
        both = lax.all_to_all(both, "frame", 0, 0, tiled=True)
        both = both.astype(f32).reshape(parts, heads, 2, half, LANES).sum(0).astype(bf16)
        return jnp.concatenate([dq[:, None], both], axis=1)

    def share_left(own, other):
        beside = swap_scene(other)
        return (own, beside, swap_frame(own, 1), swap_frame(beside, 1))

    def share_right(own):
        beside = swap_scene(own)
        return (own, beside, swap_frame(own, 1), swap_frame(beside, 1))

    def scatter(send, keep):
        bit = 2
        while True:
            held = keep.astype(f32) + swap_frame(send, bit).astype(f32)
            bit = bit * 2
            if bit >= frames:
                return held[0]
            place = lax.rem(frame // bit, 2)
            pairs = held.astype(bf16).reshape((held.shape[0] // 2, 2) + held.shape[1:])
            send = lax.dynamic_index_in_dim(pairs, 1 - place, 1, keepdims=False)
            keep = lax.dynamic_index_in_dim(pairs, place, 1, keepdims=False)

    def core_blocks(held, at, deep, pieces):
        return held[at : at + deep * pieces].reshape(pieces, 2, deep // 2, CHUNK)

    def both_halves(mine, theirs):
        first = jnp.where(core == 0, mine, theirs)
        second = jnp.where(core == 0, theirs, mine)
        return jnp.concatenate([first, second], axis=1)

    def finish(held, layout):
        own, away = [], []
        for deep, pieces, at in layout:
            blocks = core_blocks(held, at, deep, pieces)
            own.append(lax.dynamic_index_in_dim(blocks, core, 1, keepdims=False))
            away.append(lax.dynamic_index_in_dim(blocks, 1 - core, 1, keepdims=False).astype(bf16).reshape(-1, CHUNK))
        came = swap_frame(jnp.concatenate(away, axis=0), 1).astype(f32)
        at = 0
        results = []
        for (deep, pieces, _), mine in zip(layout, own):
            size = pieces * deep // 2
            theirs = came[at : at + size].reshape(pieces, deep // 2, CHUNK)
            at += size
            mine = jnp.transpose(mine, (1, 0, 2)).reshape(deep // 2, pieces * CHUNK)
            theirs = jnp.transpose(theirs, (1, 0, 2)).reshape(deep // 2, pieces * CHUNK)
            results.append(both_halves(mine, theirs))
        return results

    deep_outer = hidden // 2 // chips
    deep_rest = width // 2 // chips
    pieces_inner = hidden // 2 // CHUNK
    pieces_joint = 3 * width // 2 // CHUNK
    plan_feed = [(0, hidden // 2, 0, 0)]
    plan_feed += [
        (hidden // 2, width // 2, width + piece * CHUNK, deep_outer + piece * deep_rest)
        for piece in range(pieces_inner)
    ]
    at_mixer = deep_outer + pieces_inner * deep_rest
    plan_feed += [(hidden // 2 + width // 2, width // 2, width // 2, at_mixer)]
    plan_joint = [(0, width // 2, piece * CHUNK, piece * deep_rest) for piece in range(pieces_joint)]
    layout_feed = [(deep_outer, 1, 0), (deep_rest, pieces_inner, deep_outer), (deep_rest, 1, at_mixer)]
    layout_joint = [(deep_rest, pieces_joint, 0)]

    x0 = tokens[0]
    feed_params = (mixer_weight, mixer_bias, mixer_scale, second_gain, second_shift, inner_weight, inner_bias, outer_weight, outer_bias, outer_scale)
    back_params = (outer_scale, second_gain, mixer_scale, outer_weight, inner_weight, mixer_weight)

    own0, other0, pre0, qkv0 = joint_forward(0, False, head, meta, x0, first_gain, first_shift, pattern, joint_weight, joint_bias)
    left_joint0 = share_left(own0, other0)
    att0 = frame_forward(meta, qkv0)
    own, other, middle0, branch0, feed0, slope0, x1 = feed_forward(0, False, meta, att0, x0, *feed_params)
    left_feed0 = share_left(own, other)
    own1, other1, pre1, pack1 = joint_forward(1, True, head, meta, x1, first_gain, first_shift, pattern, joint_weight, joint_bias)
    left_joint1 = share_left(own1, other1)
    q_pack, kv_pack = to_heads(pack1)
    att_heads, att_full, att_log = scene_forward(meta, q_pack, kv_pack, half)
    att1 = exchange(att_heads.reshape(heads, half, LANES))
    own, other, middle1, branch1, feed1, slope1, layer_out = feed_forward(1, True, meta, att1, x1, *feed_params)
    left_feed1 = share_left(own, other)

    grads, g_middle1, g_att1, vector_feed1 = feed_backward(1, True, heads, meta, cotangent[0], feed1, slope1, middle1, branch1, *back_params)
    send_feed1, keep_feed1 = product("product_feed_1", plan_feed, chips, meta, left_feed1, share_right(grads))
    grad_heads = exchange(g_att1)
    dq, dk, dv = scene_backward(meta, q_pack, kv_pack, grad_heads.reshape(heads * half, LANES), att_full, att_log, half)
    g_qkv1 = from_heads(dq, dk, dv)
    grads, g1, vector_joint1 = joint_backward(1, True, head, meta, g_qkv1, pre1, x1, g_middle1, first_gain, pattern, joint_weight)
    send_joint1, keep_joint1 = product("product_joint_1", plan_joint, chips, meta, left_joint1, share_right(grads))

    grads, g_middle0, g_att0, vector_feed0 = feed_backward(0, False, heads, meta, g1, feed0, slope0, middle0, branch0, *back_params)
    send_feed0, keep_feed0 = product("product_feed_0", plan_feed, chips, meta, left_feed0, share_right(grads))
    g_qkv0 = frame_backward(meta, qkv0, g_att0)
    grads, g0, vector_joint0 = joint_backward(0, False, head, meta, g_qkv0, pre0, x0, g_middle0, first_gain, pattern, joint_weight)
    send_joint0, keep_joint0 = product("product_joint_0", plan_joint, chips, meta, left_joint0, share_right(grads))

    outer1, inner1, mixer1 = finish(scatter(send_feed1, keep_feed1), layout_feed)
    (joint1,) = finish(scatter(send_joint1, keep_joint1), layout_joint)
    outer0, inner0, mixer0 = finish(scatter(send_feed0, keep_feed0), layout_feed)
    (joint0,) = finish(scatter(send_joint0, keep_joint0), layout_joint)

    vectors = jnp.concatenate([vector_feed0, vector_joint0, vector_feed1, vector_joint1], axis=0)
    vectors = lax.psum(vectors, ("scene", "frame")).reshape(2, -1, width)
    at_joint = vector_feed0.shape[0]

    def folded(index):
        return vectors[:, at_joint + index].reshape(2, heads, head).sum(1)

    return (
        layer_out[None],
        g0[None],
        vectors[:, at_joint],
        vectors[:, at_joint + 1],
        jnp.stack([joint0, joint1]),
        vectors[:, at_joint + 2 : at_joint + 5].reshape(2, 3 * width),
        folded(5),
        folded(6),
        folded(7),
        jnp.stack([mixer0, mixer1]),
        vectors[:, 5],
        vectors[:, 4],
        vectors[:, 2],
        vectors[:, 3],
        jnp.stack([inner0, inner1]),
        vectors[:, 6:at_joint].reshape(2, hidden),
        jnp.stack([outer0, outer1]),
        vectors[:, 1],
        vectors[:, 0],
    )


def solution(mesh):
    tokens_spec = P("scene", "frame", None)
    shard = P(None, ("scene", "frame"), None)
    in_specs = (tokens_spec, P("scene", "frame")) + (P(),) * 17 + (tokens_spec,)
    out_specs = (
        tokens_spec, tokens_spec, P(), P(), shard, P(), P(), P(), P(), shard,
        P(), P(), P(), P(), shard, P(), shard, P(), P(),
    )
    body = partial(local, mesh.shape["scene"], mesh.shape["frame"])
    return jax.shard_map(body, mesh=mesh, in_specs=in_specs, out_specs=out_specs, check_vma=False)
```

time: 1990 us -> 668 us (0.34)
  waiting for transfers between devices: 1380 us -> 321 us
  matrix products: 255 us -> 0 us
  Pallas kernels: 0 us -> 197 us
  local copies, waits for them, and re-layouts: 177 us -> 17.1 us
  other arithmetic: 104 us -> 18.1 us
  starting transfers between devices: 0.37 us -> 32.6 us
  blocking collectives: 36.4 us -> 60.2 us
    reduce_scatter x6 -> x0, waiting for transfers between devices: 1290 us -> none  [the longest x1 360 us: local(): lax.psum_scatter(stacked[14], ('scene', 'frame'), scatter_dimension=1, ti...]
    dot_general x66 -> x0, matrix products: 255 us -> none  [the longest x8 43.1 us: matmul_back(): lax.dot_general(left_side, right_side, (((1,), (1,)), ((), ())), preferre...]
    ppermute x0 -> x40, waiting for transfers between devices: none -> 222 us  [the longest x32 121 us: swap_frame(): return lax.ppermute(value, 'frame', [(f, f ^ bit) for f in range(frames)])]
    pallas_call x0 -> x16, Pallas kernels: none -> 197 us  [the longest x2 33.7 us: feed_backward(): call(partial(feed_back_body, block, packed), f'feed_backward_{block}', (s...]
    reshape x14 -> x1, local copies, waits for them, and re-layouts: 73.9 us -> 1.61 us  [local(): vectors = lax.psum(vectors, ('scene', 'frame')).reshape(2, -1, width)]
    all_to_all x0 -> x3, blocking collectives: none -> 60.2 us  [the longest x2 30.2 us: exchange(): return lax.all_to_all(value, 'frame', 0, 0, tiled=True)]
    unnamed x457 -> x40, local copies, waits for them, and re-layouts: 57 us -> 9.78 us
    another operation x20 -> x14, other arithmetic: 50.2 us -> 6.95 us  [the longest x1 2.29 us: from_heads(): jnp.stack([part.reshape(heads, half, LANES) for part in (dq, dk, dv)], ax...]
  transfers between devices with their start and end apart: 9 -> 42, of which waited for: 9 -> 17; matrix products, arithmetic and copies ran while one was open for 8% -> 4% of each run, Pallas kernels for 0% -> 13%
where the time goes in v1:
time: 668 us; the launch traced here: 662 us
  waiting for transfers between devices  321 us (48%)
  Pallas kernels  197 us (29%)
  blocking collectives  60.2 us (9%)
  starting transfers between devices  32.6 us (5%)
  other arithmetic  18.1 us (3%)
  local copies, waits for them, and re-layouts  17.1 us (3%)
  between operations  15.6 us (2%)
    ppermute x32, waiting for transfers between devices, swap_frame(): return lax.ppermute(value, 'frame', [(f, f ^ bit) for f in range(frames)])  121 us
    ppermute x8, waiting for transfers between devices, swap_scene(): return lax.ppermute(value, 'scene', [(s, s ^ 1) for s in range(scenes)])  101 us
    psum x1, waiting for transfers between devices, local(): vectors = lax.psum(vectors, ('scene', 'frame')).reshape(2, -1, width)  99.7 us
    pallas_call x2, Pallas kernels, feed_backward(): call(partial(feed_back_body, block, packed), f'feed_backward_{block}', (s...  33.7 us
    pallas_call x2, Pallas kernels, feed_forward(): call(partial(feed_body, block, packed), f'feed_forward_{block}', (steps,)...  33.4 us
    pallas_call x2, Pallas kernels, joint_backward(): call(partial(joint_back_body, block, packed, head), f'joint_backward_{blo...  30.7 us
    all_to_all x2, blocking collectives, exchange(): return lax.all_to_all(value, 'frame', 0, 0, tiled=True)  30.2 us
    all_to_all x1, blocking collectives, to_heads(): everything = lax.all_to_all(value, 'frame', 0, 0, tiled=True)  30 us
  transfers between devices with their start and end apart: 42, of which 17 were waited for; matrix products, arithmetic and copies ran while one was open for 4% of the time, Pallas kernels for 13%

profile of v1, /device:TPU:0, one launch (start us, length us, event | category | flops | bytes accessed | tf_op | source)
XLA Modules:
  0.0 661.6 jit_solution(9366501155948375308)
XLA Ops:
  10.7 8.9 %joint_forward_0.1 = (bf16[144,512]{1,0:T(8,128)(2,1)}, bf16[144,512]{1,0:T(8,128)(2,1)}, f32[144,2048]{1,0:T(8,128)}, bf16[144,3072]{1,0:T(8,128)(2,1)}) custom-call(s32[4]{0:T(128)} %pad_add_fusion.meta, bf16[144,1024]{1,0:T(8,128)(2,1)} %bitcast.194, bf16[2,1024]{1,0:T(2,128)(2,1)} %gain_ref.15, bf16[2,1024]{1,0:T(2,128)(2,1)} %shift_ref.6, ...), custom_call_target="tpu_custom_call" | custom-call | flops 905969664 | bytes 8650752 | tf_op jit(solution)/shard_map/joint_forward_0/pallas_call | solution.py:231
  19.7 3.7 frame_forward.1.att_ref
  23.4 16.7 %feed_forward_0.1 = (bf16[144,3072]{1,0:T(8,128)(2,1)}, bf16[144,3072]{1,0:T(8,128)(2,1)}, f32[144,1024]{1,0:T(8,128)}, f32[144,1024]{1,0:T(8,128)}, f32[144,102...) custom-call(s32[4]{0:T(128)} %pad_add_fusion.meta, bf16[144,1024]{1,0:T(8,128)(2,1)} %frame_forward.1.att_ref, ...), custom_call_target="tpu_custom_call" | custom-call | flops 2717908992 | bytes 23560192 | tf_op jit(solution)/shard_map/feed_forward_0/pallas_call | solution.py:594
  40.1 9.6 %joint_forward_1.1 = (bf16[144,512]{1,0:T(8,128)(2,1)}, bf16[144,512]{1,0:T(8,128)(2,1)}, f32[144,2048]{1,0:T(8,128)}, bf16[16,224,128]{2,1,0:T(8,128)(2,1)}) custom-call(s32[4]{0:T(128)} %pad_add_fusion.meta, f32[144,1024]{1,0:T(8,128)} %get-tuple-element.70.x_ref, bf16[2,1024]{1,0:T(2,128)(2,1)} %gain_ref.15, bf16[2,1024]{1,0:T(2,128)(2,1)} %shift_ref.6, ...), custom_call_target="tpu_custom_call" | custom-call | flops 905969664 | bytes 8650752 | tf_op jit(solution)/shard_map/joint_forward_1/pallas_call | solution.py:231
  49.8 30.0 %all_to_all.20.q_ref.kv_ref = bf16[16,224,128]{2,1,0:T(8,128)(2,1)} all-to-all(bf16[16,224,128]{2,1,0:T(8,128)(2,1)} %get-tuple-element.71), channel_id=1, replica_groups=mesh['scene'=2,'frame'=16] {'frame'}, dimensions={0} | all-to-all | bytes 1835008 | tf_op jit(solution)/shard_map/all_to_all | solution.py:902
  79.8 13.8 %scene_forward.1 = (bf16[1152,128]{1,0:T(8,128)(2,1)}, f32[1152,128]{1,0:T(8,128)}, f32[1152,128]{1,0:T(8,128)}) custom-call(s32[4]{0:T(128)} %pad_add_fusion.meta, bf16[16,224,128]{2,1,0:T(8,128)(2,1)} %all_to_all.20.q_ref.kv_ref, bf16[16,224,128]{2,1,0:T(8,128)(2,1)} %all_to_all.20.q_ref.kv_ref), custom_call_target="tpu_custom_call" | custom-call | flops 2717908992 | bytes 2949120 | tf_op jit(solution)/shard_map/scene_forward/pallas_call | solution.py:404
  93.6 15.2 %all_to_all.21.att_ref = bf16[16,72,128]{2,1,0:T(8,128)(2,1)} all-to-all(bf16[16,72,128]{2,1,0:T(8,128)(2,1)} %bitcast.229), channel_id=1, replica_groups=mesh['scene'=2,'frame'=16] {'frame'}, dimensions={0} | all-to-all | bytes 589824 | tf_op jit(solution)/shard_map/all_to_all | solution.py:896
  108.8 16.7 %feed_forward_1.1 = (bf16[144,3072]{1,0:T(8,128)(2,1)}, bf16[144,3072]{1,0:T(8,128)(2,1)}, f32[144,1024]{1,0:T(8,128)}, f32[144,1024]{1,0:T(8,128)}, f32[144,102...) custom-call(s32[4]{0:T(128)} %pad_add_fusion.meta, bf16[16,72,128]{2,1,0:T(8,128)(2,1)} %all_to_all.21.att_ref, ...), custom_call_target="tpu_custom_call" | custom-call | flops 2717908992 | bytes 23560192 | tf_op jit(solution)/shard_map/feed_forward_1/pallas_call | solution.py:594
  125.5 16.9 %feed_backward_1.1 = (bf16[2,144,3072]{2,1,0:T(8,128)(2,1)}, f32[144,1024]{1,0:T(8,128)}, bf16[16,72,128]{2,1,0:T(8,128)(2,1)}, f32[10,1024]{1,0:T(8,128)}) custom-call(s32[4]{0:T(128)} %pad_add_fusion.meta, bf16[144,1024]{1,0:T(8,128)(2,1)} %bitcast.230, f32[144,1024]{1,0:T(8,128)} %get-tuple-element.74.feed_ref, f32[144,4096]{1,0:T(8,128)} %get-tuple-element.75.slope_ref, ...), custom_call_target="tpu_custom_call" | custom-call | flops 2717908992 | bytes 24444928 | tf_op jit(solution)/shard_map/feed_backward_1/pallas_call | solution.py:684
  142.4 15.0 %all_to_all.22 = bf16[16,72,128]{2,1,0:T(8,128)(2,1)} all-to-all(bf16[16,72,128]{2,1,0:T(8,128)(2,1)} %get-tuple-element.78), channel_id=1, replica_groups=mesh['scene'=2,'frame'=16] {'frame'}, dimensions={0} | all-to-all | bytes 589824 | tf_op jit(solution)/shard_map/all_to_all | solution.py:896
  157.4 22.9 %scene_backward.1 = (bf16[1152,128]{1,0:T(8,128)(2,1)}, bf16[1152,128]{1,0:T(8,128)(2,1)}, bf16[1152,128]{1,0:T(8,128)(2,1)}) custom-call(s32[4]{0:T(128)} %pad_add_fusion.meta, bf16[16,224,128]{2,1,0:T(8,128)(2,1)} %all_to_all.20.q_ref.kv_ref, bf16[16,224,128]{2,1,0:T(8,128)(2,1)} %all_to_all.20.q_ref.kv_ref, bf16[1152,128]{1,0:T(8,128)(2,1)} %bitcast.228, ...), custom_call_target="tpu_custom_call" | custom-call | flops 6794772480 | bytes 4423680 | tf_op jit(solution)/shard_map/scene_backward/pallas_call | solution.py:495
  180.3 2.3 pad_maximum_fusion.2
  182.6 3.6 all-to-all-start.3
  186.3 1.6 collective-permute-start.33
  188.4 1.5 collective-permute-start.10
  190.2 56.7 %collective-permute-done.30.refs_1_ = bf16[144,3072]{1,0:T(8,128)(2,1)} collective-permute-done((bf16[144,3072]{1,0:T(8,128)(2,1)}, bf16[144,3072]{1,0:T(8,128)(2,1)}, u32[]{:S(2)}, u32[]{:S(2)}) %collective-permute-start.30) | collective-permute-done | bytes 884768 | tf_op jit(solution)/shard_map/ppermute | solution.py:887
  247.8 11.4 %joint_backward_1.1 = (bf16[2,144,1536]{2,1,0:T(8,128)(2,1)}, f32[144,1024]{1,0:T(8,128)}, f32[8,1024]{1,0:T(8,128)}) custom-call(s32[4]{0:T(128)} %pad_add_fusion.meta, bf16[16,3,72,128]{3,2,1,0:T(8,128)(2,1)} %copy-done, f32[144,2048]{1,0:T(8,128)} %get-tuple-element.84.pre_ref, f32[144,1024]{1,0:T(8,128)} %get-tuple-element.70.x_ref, ...), custom_call_target="tpu_custom_call" | custom-call | flops 905969664 | bytes 10715136 | tf_op jit(solution)/shard_map/joint_backward_1/pallas_call | solution.py:802
  259.2 1.6 collective-permute-start.13
  261.3 23.4 %collective-permute-done.refs_1_ = bf16[144,512]{1,0:T(8,128)(2,1)S(1)} collective-permute-done((bf16[144,512]{1,0:T(8,128)(2,1)}, bf16[144,512]{1,0:T(8,128)(2,1)S(1)}, u32[]{:S(2)}, u32[]{:S(2)}) %collective-permute-start) | collective-permute-done | bytes 147488 | tf_op jit(solution)/shard_map/ppermute | solution.py:887
  284.7 1.6 collective-permute-done.1.refs_2_
  288.5 16.8 %feed_backward_0.1 = (bf16[2,144,3072]{2,1,0:T(8,128)(2,1)}, f32[144,1024]{1,0:T(8,128)}, bf16[144,1024]{1,0:T(8,128)(2,1)}, f32[10,1024]{1,0:T(8,128)}) custom-call(s32[4]{0:T(128)} %pad_add_fusion.meta, f32[144,1024]{1,0:T(8,128)} %get-tuple-element.86.g_ref, f32[144,1024]{1,0:T(8,128)} %get-tuple-element.87.feed_ref, ...), custom_call_target="tpu_custom_call" | custom-call | flops 2717908992 | bytes 24444928 | tf_op jit(solution)/shard_map/feed_backward_0/pallas_call | solution.py:684
  305.3 10.1 %frame_backward.1.g_ref = f32[144,3072]{1,0:T(8,128)} custom-call(s32[4]{0:T(128)} %pad_add_fusion.meta, bf16[144,3072]{1,0:T(8,128)(2,1)} %get-tuple-element.69.qkv_ref, bf16[144,1024]{1,0:T(8,128)(2,1)} %get-tuple-element.91.grad_ref), custom_call_target="tpu_custom_call" | custom-call | flops 212336640 | bytes 2949120 | tf_op jit(solution)/shard_map/frame_backward/pallas_call | solution.py:338
  315.5 19.3 %joint_backward_0.1 = (bf16[2,144,1536]{2,1,0:T(8,128)(2,1)}, bf16[144,1024]{1,0:T(8,128)(2,1)}, f32[8,1024]{1,0:T(8,128)}) custom-call(s32[4]{0:T(128)} %pad_add_fusion.meta, f32[144,3072]{1,0:T(8,128)} %frame_backward.1.g_ref, f32[144,2048]{1,0:T(8,128)} %get-tuple-element.92.pre_ref, bf16[144,1024]{1,0:T(8,128)(2,1)} %bitcast.196, ...), custom_call_target="tpu_custom_call" | custom-call | flops 905969664 | bytes 10715136 | tf_op jit(solution)/shard_map/joint_backward_0/pallas_call | solution.py:802
  334.8 1.6 collective-permute-start.3
  337.0 20.6 %collective-permute-done.3.refs_5_ = bf16[2,144,1536]{2,1,0:T(8,128)(2,1)S(1)} collective-permute-done((bf16[2,144,1536]{2,1,0:T(8,128)(2,1)}, bf16[2,144,1536]{2,1,0:T(8,128)(2,1)S(1)}, u32[]{:S(2)}, u32[]{:S(2)}) %collective-permute-start.3) | collective-permute-done | bytes 884768 | tf_op jit(solution)/shard_map/ppermute | solution.py:887
  359.0 1.6 pad_maximum_fusion.7
  360.6 1.6 reshape.261
  362.2 4.9 product_joint_1.1
  367.3 1.8 collective-permute-start.16
  369.2 9.8 %product_feed_1.1 = (bf16[4,576,512]{2,1,0:T(8,128)(2,1)}, bf16[4,576,512]{2,1,0:T(8,128)(2,1)}) custom-call(s32[4]{0:T(128)} %pad_add_fusion.meta, bf16[144,3072]{1,0:T(8,128)(2,1)} %get-tuple-element.114.refs_0_, bf16[144,3072]{1,0:T(8,128)(2,1)} %collective-permute-done.30.refs_1_, bf16[144,3072]{1,0:T(8,128)(2,1)} %collective-permute-done.31.refs_2_, ...), custom_call_target="tpu_custom_call" | custom-call | flops 2717908992 | bytes 11796480 | tf_op jit(solution)/shard_map/product_feed_1/pallas_call | solution.py:855
  378.9 1.6 collective-permute-start.20
  380.8 4.9 product_joint_0.1
  385.8 1.8 collective-permute-start.6
  387.5 99.7 %all-reduce.2.cloned.1.call-done = f32[2,18,1024]{2,1,0:T(8,128)} async-done(((f32[2,18,1024]{2,1,0:T(8,128)}), f32[2,18,1024]{2,1,0:T(8,128)}) %all-reduce.2.cloned.1.call-update) | async-done | bytes 147472 | tf_op jit(solution)/shard_map/psum | solution.py:1015
  490.4 3.3 collective-permute-start.17
  495.1 8.0 %collective-permute-done.17 = bf16[2,192,512]{2,1,0:T(8,128)(2,1)S(1)} collective-permute-done((bf16[2,192,512]{2,1,0:T(8,128)(2,1)S(1)}, bf16[2,192,512]{2,1,0:T(8,128)(2,1)S(1)}, u32[]{:S(2)}, u32[]{:S(2)}) %collective-permute-start.17) | collective-permute-done | bytes 393248 | tf_op jit(solution)/shard_map/ppermute | solution.py:890
  503.1 1.7 collective-permute-start.7
  515.7 9.2 %collective-permute-done.18 = bf16[1,192,512]{2,1,0:T(8,128)(2,1)S(1)} collective-permute-done((bf16[1,192,512]{2,1,0:T(8,128)(2,1)S(1)}, bf16[1,192,512]{2,1,0:T(8,128)(2,1)S(1)}, u32[]{:S(2)}, u32[]{:S(2)}) %collective-permute-start.18) | collective-permute-done | bytes 196640 | tf_op jit(solution)/shard_map/ppermute | solution.py:890
  525.1 2.4 add_convert_fusion
  528.7 2.1 collective-permute-start.37
  530.7 10.0 %product_feed_0.1 = (bf16[4,576,512]{2,1,0:T(8,128)(2,1)}, bf16[4,576,512]{2,1,0:T(8,128)(2,1)}) custom-call(s32[4]{0:T(128)} %pad_add_fusion.meta, bf16[144,3072]{1,0:T(8,128)(2,1)} %get-tuple-element.109.refs_0_, bf16[144,3072]{1,0:T(8,128)(2,1)} %collective-permute-done.20.refs_1_, bf16[144,3072]{1,0:T(8,128)(2,1)} %collective-permute-done.21.refs_2_, ...), custom_call_target="tpu_custom_call" | custom-call | flops 2717908992 | bytes 11796480 | tf_op jit(solution)/shard_map/product_feed_0/pallas_call | solution.py:855
  544.0 17.6 %collective-permute-done.37 = bf16[2,576,512]{2,1,0:T(8,128)(2,1)} collective-permute-done((bf16[2,576,512]{2,1,0:T(8,128)(2,1)}, bf16[2,576,512]{2,1,0:T(8,128)(2,1)}, u32[]{:S(2)}, u32[]{:S(2)}) %collective-permute-start.37) | collective-permute-done | bytes 1179680 | tf_op jit(solution)/shard_map/ppermute | solution.py:890
  561.5 1.6 fusion
  563.7 27.8 %collective-permute-done.38 = bf16[1,576,512]{2,1,0:T(8,128)(2,1)S(1)} collective-permute-done((bf16[1,576,512]{2,1,0:T(8,128)(2,1)S(1)}, bf16[1,576,512]{2,1,0:T(8,128)(2,1)S(1)}, u32[]{:S(2)}, u32[]{:S(2)}) %collective-permute-start.38) | collective-permute-done | bytes 589856 | tf_op jit(solution)/shard_map/ppermute | solution.py:890
  591.7 2.3 collective-permute-done.26
  597.2 24.7 %collective-permute-done.27 = bf16[2,576,512]{2,1,0:T(8,128)(2,1)S(1)} collective-permute-done((bf16[2,576,512]{2,1,0:T(8,128)(2,1)S(1)}, bf16[2,576,512]{2,1,0:T(8,128)(2,1)S(1)}, u32[]{:S(2)}, u32[]{:S(2)}) %collective-permute-start.27) | collective-permute-done | bytes 1179680 | tf_op jit(solution)/shard_map/ppermute | solution.py:890
  624.0 25.3 %collective-permute-done.28 = bf16[1,576,512]{2,1,0:T(8,128)(2,1)S(1)} collective-permute-done((bf16[1,576,512]{2,1,0:T(8,128)(2,1)S(1)}, bf16[1,576,512]{2,1,0:T(8,128)(2,1)S(1)}, u32[]{:S(2)}, u32[]{:S(2)}) %collective-permute-start.28) | collective-permute-done | bytes 589856 | tf_op jit(solution)/shard_map/ppermute | solution.py:890
  649.8 1.5 collective-permute-done.29
  (178 shorter events, 38.9 us)
Async XLA Ops:
  182.6 64.3 %all-to-all-start.3 = ((bf16[16,3,72,128]{3,2,1,0:T(8,128)(2,1)}), bf16[16,3,72,128]{3,2,1,0:T(8,128)(2,1)S(1)}, u32[]{:S(2)}, u32[]{:S(2)}) async-start(bf16[16,3,72,128]{3,2,1,0:T(8,128)(2,1)} %pad_maximum_fusion.2), calls=%async_computation.3 | async-start | bytes 1769472 | tf_op jit(solution)/shard_map/all_to_all | solution.py:896
  186.2 301.0 %all-reduce.2.cloned.1.call-start = ((), (), s32[]{:S(2)}) async-start(), calls=%async_computation.4 | async-start | bytes 393216 | tf_op jit(solution)/shard_map/psum | solution.py:1015
  186.3 101.7 %collective-permute-start.33 = (bf16[2,144,3072]{2,1,0:T(8,128)(2,1)S(1)}, bf16[2,144,3072]{2,1,0:T(8,128)(2,1)}, u32[]{:S(2)}, u32[]{:S(2)}) collective-permute-start(bf16[2,144,3072]{2,1,0:T(8,128)(2,1)S(1)} %copy-done.3), channel_id=1, source_target_pairs={{0,16},{16,0},{1,17},{17,1},{2,18},{18,2},{3,19},{19,3},{4,20},{20... | collective-permute-start | bytes 5308424 | tf_op jit(solution)/shard_map/ppermute | solution.py:887
  187.9 59.0 %collective-permute-start.30 = (bf16[144,3072]{1,0:T(8,128)(2,1)}, bf16[144,3072]{1,0:T(8,128)(2,1)}, u32[]{:S(2)}, u32[]{:S(2)}) collective-permute-start(bf16[144,3072]{1,0:T(8,128)(2,1)} %get-tuple-element.115), channel_id=1, source_target_pairs={{0,16},{16,0},{1,17},{17,1},{2,18},{18,2},{3,19},{19,3},{4,20},{20... | collective-permute-start | bytes 2654216 | tf_op jit(solution)/shard_map/ppermute | solution.py:887
  188.4 100.0 %collective-permute-start.31 = (bf16[144,3072]{1,0:T(8,128)(2,1)S(1)}, bf16[144,3072]{1,0:T(8,128)(2,1)}, u32[]{:S(2)}, u32[]{:S(2)}) collective-permute-start(bf16[144,3072]{1,0:T(8,128)(2,1)S(1)} %copy-done.7), channel_id=1, source_target_pairs={{0,1},{1,0},{2,3},{3,2},{4,5},{5,4},{6,7},{7,6},{8,9},{9,8},{10,11... | collective-permute-start | bytes 2654216 | tf_op jit(solution)/shard_map/ppermute | solution.py:890
  188.4 70.8 %collective-permute-start.10 = (bf16[144,512]{1,0:T(8,128)(2,1)}, bf16[144,512]{1,0:T(8,128)(2,1)}, u32[]{:S(2)}, u32[]{:S(2)}) collective-permute-start(bf16[144,512]{1,0:T(8,128)(2,1)} %get-tuple-element.105), channel_id=1, source_target_pairs={{0,16},{16,0},{1,17},{17,1},{2,18},{18,2},{3,19},{19,3},{4,20},{20... | collective-permute-start | bytes 442376 | tf_op jit(solution)/shard_map/ppermute | solution.py:887
  189.9 70.8 %collective-permute-start.11 = (bf16[144,512]{1,0:T(8,128)(2,1)}, bf16[144,512]{1,0:T(8,128)(2,1)}, u32[]{:S(2)}, u32[]{:S(2)}) collective-permute-start(bf16[144,512]{1,0:T(8,128)(2,1)} %get-tuple-element.104.refs_0_), channel_id=1, source_target_pairs={{0,1},{1,0},{2,3},{3,2},{4,5},{5,4},{6,7},{7,6},{8,9},{9,8},{10,11... | collective-permute-start | bytes 442376 | tf_op jit(solution)/shard_map/ppermute | solution.py:890
  246.9 87.9 %collective-permute-start.32 = (bf16[144,3072]{1,0:T(8,128)(2,1)}, bf16[144,3072]{1,0:T(8,128)(2,1)}, u32[]{:S(2)}, u32[]{:S(2)}) collective-permute-start(bf16[144,3072]{1,0:T(8,128)(2,1)} %collective-permute-done.30.refs_1_), channel_id=1, source_target_pairs={{0,1},{1,0},{2,3},{3,2},{4,5},{5,4},{6,7},{7,6},{8,9},{9,8},{10,11... | collective-permute-start | bytes 2654216 | tf_op jit(solution)/shard_map/ppermute | solution.py:890
  259.2 77.3 %collective-permute-start.13 = (bf16[2,144,1536]{2,1,0:T(8,128)(2,1)}, bf16[2,144,1536]{2,1,0:T(8,128)(2,1)S(1)}, u32[]{:S(2)}, u32[]{:S(2)}) collective-permute-start(bf16[2,144,1536]{2,1,0:T(8,128)(2,1)} %get-tuple-element.106.refs_4_), channel_id=1, source_target_pairs={{0,16},{16,0},{1,17},{17,1},{2,18},{18,2},{3,19},{19,3},{4,20},{20... | collective-permute-start | bytes 2654216 | tf_op jit(solution)/shard_map/ppermute | solution.py:887
  260.8 23.9 %collective-permute-start = (bf16[144,512]{1,0:T(8,128)(2,1)}, bf16[144,512]{1,0:T(8,128)(2,1)S(1)}, u32[]{:S(2)}, u32[]{:S(2)}) collective-permute-start(bf16[144,512]{1,0:T(8,128)(2,1)} %get-tuple-element.100), channel_id=1, source_target_pairs={{0,16},{16,0},{1,17},{17,1},{2,18},{18,2},{3,19},{19,3},{4,20},{20... | collective-permute-start | bytes 442376 | tf_op jit(solution)/shard_map/ppermute | solution.py:887
  284.7 1.6 collective-permute-start.1
  286.2 1.6 collective-permute-start.12
  287.8 79.4 %collective-permute-start.34 = (bf16[2,144,3072]{2,1,0:T(8,128)(2,1)S(1)}, bf16[2,144,3072]{2,1,0:T(8,128)(2,1)}, u32[]{:S(2)}, u32[]{:S(2)}) collective-permute-start(bf16[2,144,3072]{2,1,0:T(8,128)(2,1)S(1)} %copy-done.3), channel_id=1, source_target_pairs={{0,1},{1,0},{2,3},{3,2},{4,5},{5,4},{6,7},{7,6},{8,9},{9,8},{10,11... | collective-permute-start | bytes 5308424 | tf_op jit(solution)/shard_map/ppermute | solution.py:890
  288.0 79.3 %collective-permute-start.35 = (bf16[2,144,3072]{2,1,0:T(8,128)(2,1)}, bf16[2,144,3072]{2,1,0:T(8,128)(2,1)}, u32[]{:S(2)}, u32[]{:S(2)}) collective-permute-start(bf16[2,144,3072]{2,1,0:T(8,128)(2,1)} %collective-permute-done.33.refs_5_), channel_id=1, source_target_pairs={{0,1},{1,0},{2,3},{3,2},{4,5},{5,4},{6,7},{7,6},{8,9},{9,8},{10,11... | collective-permute-start | bytes 5308424 | tf_op jit(solution)/shard_map/ppermute | solution.py:890
  288.4 48.1 %collective-permute-start.14 = (bf16[2,144,1536]{2,1,0:T(8,128)(2,1)}, bf16[2,144,1536]{2,1,0:T(8,128)(2,1)}, u32[]{:S(2)}, u32[]{:S(2)}) collective-permute-start(bf16[2,144,1536]{2,1,0:T(8,128)(2,1)} %get-tuple-element.106.refs_4_), channel_id=1, source_target_pairs={{0,1},{1,0},{2,3},{3,2},{4,5},{5,4},{6,7},{7,6},{8,9},{9,8},{10,11... | collective-permute-start | bytes 2654216 | tf_op jit(solution)/shard_map/ppermute | solution.py:890
  334.8 22.8 %collective-permute-start.3 = (bf16[2,144,1536]{2,1,0:T(8,128)(2,1)}, bf16[2,144,1536]{2,1,0:T(8,128)(2,1)S(1)}, u32[]{:S(2)}, u32[]{:S(2)}) collective-permute-start(bf16[2,144,1536]{2,1,0:T(8,128)(2,1)} %get-tuple-element.101.refs_4_), channel_id=1, source_target_pairs={{0,16},{16,0},{1,17},{17,1},{2,18},{18,2},{3,19},{19,3},{4,20},{20... | collective-permute-start | bytes 2654216 | tf_op jit(solution)/shard_map/ppermute | solution.py:887
  336.4 25.8 %copy-start.4 = (bf16[2,144,1536]{2,1,0:T(8,128)(2,1)}, bf16[2,144,1536]{2,1,0:T(8,128)(2,1)S(1)}, u32[]{:S(2)}) copy-start(bf16[2,144,1536]{2,1,0:T(8,128)(2,1)S(1)} %collective-permute-done.13.refs_5_) | copy-start | bytes 2654212
  336.4 21.1 %collective-permute-start.15 = (bf16[2,144,1536]{2,1,0:T(8,128)(2,1)S(1)}, bf16[2,144,1536]{2,1,0:T(8,128)(2,1)S(1)}, u32[]{:S(2)}, u32[]{:S(2)}) collective-permute-start(bf16[2,144,1536]{2,1,0:T(8,128)(2,1)S(1)} %collective-permute-done.13.refs_5_), channel_id=1, source_target_pairs={{0,1},{1,0},{2,3},{3,2},{4,5},{5,4},{6,7},{7,6},{8,9},{9,8},{10,11... | collective-permute-start | bytes 2654216 | tf_op jit(solution)/shard_map/ppermute | solution.py:890
  336.5 153.0 %collective-permute-start.23 = (bf16[2,144,3072]{2,1,0:T(8,128)(2,1)}, bf16[2,144,3072]{2,1,0:T(8,128)(2,1)}, u32[]{:S(2)}, u32[]{:S(2)}) collective-permute-start(bf16[2,144,3072]{2,1,0:T(8,128)(2,1)} %get-tuple-element.111.refs_4_), channel_id=1, source_target_pairs={{0,16},{16,0},{1,17},{17,1},{2,18},{18,2},{3,19},{19,3},{4,20},{20... | collective-permute-start | bytes 5308424 | tf_op jit(solution)/shard_map/ppermute | solution.py:887
  357.6 9.6 %copy-start.5 = (bf16[2,144,1536]{2,1,0:T(8,128)(2,1)}, bf16[2,144,1536]{2,1,0:T(8,128)(2,1)S(1)}, u32[]{:S(2)}) copy-start(bf16[2,144,1536]{2,1,0:T(8,128)(2,1)S(1)} %collective-permute-done.3.refs_5_) | copy-start | bytes 2654212
  357.6 23.0 %collective-permute-start.4 = (bf16[2,144,1536]{2,1,0:T(8,128)(2,1)}, bf16[2,144,1536]{2,1,0:T(8,128)(2,1)}, u32[]{:S(2)}, u32[]{:S(2)}) collective-permute-start(bf16[2,144,1536]{2,1,0:T(8,128)(2,1)} %get-tuple-element.101.refs_4_), channel_id=1, source_target_pairs={{0,1},{1,0},{2,3},{3,2},{4,5},{5,4},{6,7},{7,6},{8,9},{9,8},{10,11... | collective-permute-start | bytes 2654216 | tf_op jit(solution)/shard_map/ppermute | solution.py:890
  358.5 22.3 %collective-permute-start.5 = (bf16[2,144,1536]{2,1,0:T(8,128)(2,1)S(1)}, bf16[2,144,1536]{2,1,0:T(8,128)(2,1)}, u32[]{:S(2)}, u32[]{:S(2)}) collective-permute-start(bf16[2,144,1536]{2,1,0:T(8,128)(2,1)S(1)} %collective-permute-done.3.refs_5_), channel_id=1, source_target_pairs={{0,1},{1,0},{2,3},{3,2},{4,5},{5,4},{6,7},{7,6},{8,9},{9,8},{10,11... | collective-permute-start | bytes 2654216 | tf_op jit(solution)/shard_map/ppermute | solution.py:890
  367.2 11.7 %collective-permute-start.2 = (bf16[144,512]{1,0:T(8,128)(2,1)}, bf16[144,512]{1,0:T(8,128)(2,1)S(1)}, u32[]{:S(2)}, u32[]{:S(2)}) collective-permute-start(bf16[144,512]{1,0:T(8,128)(2,1)} %copy-done.10), channel_id=1, source_target_pairs={{0,1},{1,0},{2,3},{3,2},{4,5},{5,4},{6,7},{7,6},{8,9},{9,8},{10,11... | collective-permute-start | bytes 442376 | tf_op jit(solution)/shard_map/ppermute | solution.py:890
  367.3 122.3 %collective-permute-start.16 = (bf16[4,192,512]{2,1,0:T(8,128)(2,1)}, bf16[4,192,512]{2,1,0:T(8,128)(2,1)S(1)}, u32[]{:S(2)}, u32[]{:S(2)}) collective-permute-start(bf16[4,192,512]{2,1,0:T(8,128)(2,1)} %get-tuple-element.108), channel_id=1, source_target_pairs={{0,2},{1,3},{2,0},{3,1},{4,6},{5,7},{6,4},{7,5},{8,10},{9,11},{10,... | collective-permute-start | bytes 2359304 | tf_op jit(solution)/shard_map/ppermute | solution.py:890
  378.9 136.7 %collective-permute-start.20 = (bf16[144,3072]{1,0:T(8,128)(2,1)}, bf16[144,3072]{1,0:T(8,128)(2,1)}, u32[]{:S(2)}, u32[]{:S(2)}) collective-permute-start(bf16[144,3072]{1,0:T(8,128)(2,1)} %get-tuple-element.110), channel_id=1, source_target_pairs={{0,16},{16,0},{1,17},{17,1},{2,18},{18,2},{3,19},{19,3},{4,20},{20... | collective-permute-start | bytes 2654216 | tf_op jit(solution)/shard_map/ppermute | solution.py:887
  380.6 109.6 %copy-start.8 = (bf16[4,192,512]{2,1,0:T(8,128)(2,1)S(1)}, bf16[4,192,512]{2,1,0:T(8,128)(2,1)}, u32[]{:S(2)}) copy-start(bf16[4,192,512]{2,1,0:T(8,128)(2,1)} %get-tuple-element.107) | copy-start | bytes 2359300
  380.6 144.5 %collective-permute-start.36 = (bf16[4,576,512]{2,1,0:T(8,128)(2,1)}, bf16[4,576,512]{2,1,0:T(8,128)(2,1)}, u32[]{:S(2)}, u32[]{:S(2)}) collective-permute-start(bf16[4,576,512]{2,1,0:T(8,128)(2,1)} %get-tuple-element.118), channel_id=1, source_target_pairs={{0,2},{1,3},{2,0},{3,1},{4,6},{5,7},{6,4},{7,5},{8,10},{9,11},{10,... | collective-permute-start | bytes 7077896 | tf_op jit(solution)/shard_map/ppermute | solution.py:890
  385.8 108.0 %copy-start.9 = (bf16[4,192,512]{2,1,0:T(8,128)(2,1)S(1)}, bf16[4,192,512]{2,1,0:T(8,128)(2,1)}, u32[]{:S(2)}) copy-start(bf16[4,192,512]{2,1,0:T(8,128)(2,1)} %get-tuple-element.102) | copy-start | bytes 2359300
  385.8 104.6 %collective-permute-start.6 = (bf16[4,192,512]{2,1,0:T(8,128)(2,1)}, bf16[4,192,512]{2,1,0:T(8,128)(2,1)}, u32[]{:S(2)}, u32[]{:S(2)}) collective-permute-start(bf16[4,192,512]{2,1,0:T(8,128)(2,1)} %get-tuple-element.103), channel_id=1, source_target_pairs={{0,2},{1,3},{2,0},{3,1},{4,6},{5,7},{6,4},{7,5},{8,10},{9,11},{10,... | collective-permute-start | bytes 2359304 | tf_op jit(solution)/shard_map/ppermute | solution.py:890
  489.5 41.2 %collective-permute-start.24 = (bf16[2,144,3072]{2,1,0:T(8,128)(2,1)}, bf16[2,144,3072]{2,1,0:T(8,128)(2,1)}, u32[]{:S(2)}, u32[]{:S(2)}) collective-permute-start(bf16[2,144,3072]{2,1,0:T(8,128)(2,1)} %get-tuple-element.111.refs_4_), channel_id=1, source_target_pairs={{0,1},{1,0},{2,3},{3,2},{4,5},{5,4},{6,7},{7,6},{8,9},{9,8},{10,11... | collective-permute-start | bytes 5308424 | tf_op jit(solution)/shard_map/ppermute | solution.py:890
  489.6 41.1 %collective-permute-start.25 = (bf16[2,144,3072]{2,1,0:T(8,128)(2,1)}, bf16[2,144,3072]{2,1,0:T(8,128)(2,1)}, u32[]{:S(2)}, u32[]{:S(2)}) collective-permute-start(bf16[2,144,3072]{2,1,0:T(8,128)(2,1)} %collective-permute-done.23.refs_5_), channel_id=1, source_target_pairs={{0,1},{1,0},{2,3},{3,2},{4,5},{5,4},{6,7},{7,6},{8,9},{9,8},{10,11... | collective-permute-start | bytes 5308424 | tf_op jit(solution)/shard_map/ppermute | solution.py:890
  490.4 12.7 %collective-permute-start.17 = (bf16[2,192,512]{2,1,0:T(8,128)(2,1)S(1)}, bf16[2,192,512]{2,1,0:T(8,128)(2,1)S(1)}, u32[]{:S(2)}, u32[]{:S(2)}) collective-permute-start(bf16[2,192,512]{2,1,0:T(8,128)(2,1)S(1)} %dynamic-slice_bitcast_fusion.2), channel_id=1, source_target_pairs={{0,4},{1,5},{2,6},{3,7},{4,0},{5,1},{6,2},{7,3},{8,12},{9,13},{10,... | collective-permute-start | bytes 1179656 | tf_op jit(solution)/shard_map/ppermute | solution.py:890
  503.1 10.9 %collective-permute-start.7 = (bf16[2,192,512]{2,1,0:T(8,128)(2,1)S(1)}, bf16[2,192,512]{2,1,0:T(8,128)(2,1)S(1)}, u32[]{:S(2)}, u32[]{:S(2)}) collective-permute-start(bf16[2,192,512]{2,1,0:T(8,128)(2,1)S(1)} %dynamic-slice_bitcast_fusion.3), channel_id=1, source_target_pairs={{0,4},{1,5},{2,6},{3,7},{4,0},{5,1},{6,2},{7,3},{8,12},{9,13},{10,... | collective-permute-start | bytes 1179656 | tf_op jit(solution)/shard_map/ppermute | solution.py:890
  513.8 11.3 %copy-start.1 = (bf16[4,576,512]{2,1,0:T(8,128)(2,1)S(1)}, bf16[4,576,512]{2,1,0:T(8,128)(2,1)}, u32[]{:S(2)}) copy-start(bf16[4,576,512]{2,1,0:T(8,128)(2,1)} %get-tuple-element.117) | copy-start | bytes 7077892
  514.0 10.9 %collective-permute-start.18 = (bf16[1,192,512]{2,1,0:T(8,128)(2,1)S(1)}, bf16[1,192,512]{2,1,0:T(8,128)(2,1)S(1)}, u32[]{:S(2)}, u32[]{:S(2)}) collective-permute-start(bf16[1,192,512]{2,1,0:T(8,128)(2,1)S(1)} %constant_dynamic-slice_fusion.2), channel_id=1, source_target_pairs={{0,8},{1,9},{2,10},{3,11},{4,12},{5,13},{6,14},{7,15},{8,0},{9,1},... | collective-permute-start | bytes 589832 | tf_op jit(solution)/shard_map/ppermute | solution.py:890
  515.6 13.0 %collective-permute-start.21 = (bf16[144,3072]{1,0:T(8,128)(2,1)}, bf16[144,3072]{1,0:T(8,128)(2,1)}, u32[]{:S(2)}, u32[]{:S(2)}) collective-permute-start(bf16[144,3072]{1,0:T(8,128)(2,1)} %get-tuple-element.109.refs_0_), channel_id=1, source_target_pairs={{0,1},{1,0},{2,3},{3,2},{4,5},{5,4},{6,7},{7,6},{8,9},{9,8},{10,11... | collective-permute-start | bytes 2654216 | tf_op jit(solution)/shard_map/ppermute | solution.py:890
  525.0 5.8 collective-permute-start.22
  525.0 17.2 %collective-permute-start.8 = (bf16[1,192,512]{2,1,0:T(8,128)(2,1)S(1)}, bf16[1,192,512]{2,1,0:T(8,128)(2,1)S(1)}, u32[]{:S(2)}, u32[]{:S(2)}) collective-permute-start(bf16[1,192,512]{2,1,0:T(8,128)(2,1)S(1)} %constant_dynamic-slice_fusion.3), channel_id=1, source_target_pairs={{0,8},{1,9},{2,10},{3,11},{4,12},{5,13},{6,14},{7,15},{8,0},{9,1},... | collective-permute-start | bytes 589832 | tf_op jit(solution)/shard_map/ppermute | solution.py:890
  528.7 32.9 %collective-permute-start.37 = (bf16[2,576,512]{2,1,0:T(8,128)(2,1)}, bf16[2,576,512]{2,1,0:T(8,128)(2,1)}, u32[]{:S(2)}, u32[]{:S(2)}) collective-permute-start(bf16[2,576,512]{2,1,0:T(8,128)(2,1)} %dynamic-slice_bitcast_fusion), channel_id=1, source_target_pairs={{0,4},{1,5},{2,6},{3,7},{4,0},{5,1},{6,2},{7,3},{8,12},{9,13},{10,... | collective-permute-start | bytes 3538952 | tf_op jit(solution)/shard_map/ppermute | solution.py:890
  540.7 53.3 %collective-permute-start.26 = (bf16[4,576,512]{2,1,0:T(8,128)(2,1)}, bf16[4,576,512]{2,1,0:T(8,128)(2,1)S(1)}, u32[]{:S(2)}, u32[]{:S(2)}) collective-permute-start(bf16[4,576,512]{2,1,0:T(8,128)(2,1)} %get-tuple-element.113), channel_id=1, source_target_pairs={{0,2},{1,3},{2,0},{3,1},{4,6},{5,7},{6,4},{7,5},{8,10},{9,11},{10,... | collective-permute-start | bytes 7077896 | tf_op jit(solution)/shard_map/ppermute | solution.py:890
  542.2 1.4 collective-permute-start.19
  542.4 1.5 collective-permute-start.9
  563.2 28.3 %collective-permute-start.38 = (bf16[1,576,512]{2,1,0:T(8,128)(2,1)S(1)}, bf16[1,576,512]{2,1,0:T(8,128)(2,1)S(1)}, u32[]{:S(2)}, u32[]{:S(2)}) collective-permute-start(bf16[1,576,512]{2,1,0:T(8,128)(2,1)S(1)} %constant_dynamic-slice_fusion), channel_id=1, source_target_pairs={{0,8},{1,9},{2,10},{3,11},{4,12},{5,13},{6,14},{7,15},{8,0},{9,1},... | collective-permute-start | bytes 1769480 | tf_op jit(solution)/shard_map/ppermute | solution.py:890
  563.6 30.4 %copy-start.2 = (bf16[4,576,512]{2,1,0:T(8,128)(2,1)S(1)}, bf16[4,576,512]{2,1,0:T(8,128)(2,1)}, u32[]{:S(2)}) copy-start(bf16[4,576,512]{2,1,0:T(8,128)(2,1)} %get-tuple-element.112) | copy-start | bytes 7077892
  594.8 27.0 %collective-permute-start.27 = (bf16[2,576,512]{2,1,0:T(8,128)(2,1)S(1)}, bf16[2,576,512]{2,1,0:T(8,128)(2,1)S(1)}, u32[]{:S(2)}, u32[]{:S(2)}) collective-permute-start(bf16[2,576,512]{2,1,0:T(8,128)(2,1)S(1)} %dynamic-slice_bitcast_fusion.1), channel_id=1, source_target_pairs={{0,4},{1,5},{2,6},{3,7},{4,0},{5,1},{6,2},{7,3},{8,12},{9,13},{10,... | collective-permute-start | bytes 3538952 | tf_op jit(solution)/shard_map/ppermute | solution.py:890
  595.4 1.6 collective-permute-start.39
  622.3 27.0 %collective-permute-start.28 = (bf16[1,576,512]{2,1,0:T(8,128)(2,1)S(1)}, bf16[1,576,512]{2,1,0:T(8,128)(2,1)S(1)}, u32[]{:S(2)}, u32[]{:S(2)}) collective-permute-start(bf16[1,576,512]{2,1,0:T(8,128)(2,1)S(1)} %constant_dynamic-slice_fusion.1), channel_id=1, source_target_pairs={{0,8},{1,9},{2,10},{3,11},{4,12},{5,13},{6,14},{7,15},{8,0},{9,1},... | collective-permute-start | bytes 1769480 | tf_op jit(solution)/shard_map/ppermute | solution.py:890
  649.7 1.6 collective-permute-start.29
  (8 other events, 24.5 us)
Sparse Core Ops, SparseCore 0:
  362.4 124.8 all-reduce.1
